TPU v7x, 32 devices: a whole 2x2x4 slice. The times are simulated.
32 devices in a mesh: groups: 2 (over x), slab: 16 (over z, y, core).
Axes of the slice: x: 2, y: 2, z: 4, core: 2. Of those that a mesh axis runs over, the one named last changes fastest.
Arguments:
- melt_speeds: float32 [3, 64, 32, 512], P(None, ('groups', 'slab')), parts along dimension 1, may hold values from -3 to 3
- heat_state: float32 [64, 32, 512], P(('groups', 'slab')), parts along dimension 0, may hold values from -4 to 4
- eddy_quantities: float32 [2, 64, 32, 512], P(None, ('groups', 'slab')), parts along dimension 1, may hold values from 0.02 to 1
- zone_labels: int32 [32, 16, 256], P(('groups', 'slab')), parts along dimension 0, may hold values from 0 to 7
- zone_resistivity_inverse: float32 [8], replicated, may hold values from 0.05 to 0.4
- imposed_induction: float32 [3, 512, 16, 16], P(None, ('groups', 'slab')), parts along dimension 1, may hold values from -4 to 4
- winding_current: float32 [3, 512, 16, 16], P(None, ('groups', 'slab')), parts along dimension 1, may hold values from -4 to 4
- window_entry_induction_guess: float32 [3, 512, 16, 16], P(None, ('groups', 'slab')), parts along dimension 1, may hold values from 1 to 4
Outputs:
- velocity_out: float32 [3, 64, 32, 512], P(None, ('groups', 'slab')), parts along dimension 1
- temperature_out: float32 [64, 32, 512], P(('groups', 'slab')), parts along dimension 0
- turbulence_out: float32 [2, 64, 32, 512], P(None, ('groups', 'slab')), parts along dimension 1
- potential: float32 [3, 512, 16, 16], P(None, ('groups', 'slab')), parts along dimension 1
There are 2 independent parts, one for each index of `groups`. A program takes and returns all parts, laid end to end along the dimension named above; an argument that names none is the same for every part. Nothing has to cross between parts.
Inputs may be any that keep to these rules, and one draw needn't show every extreme that they name: `zone_labels`: region number of each coarse block.
All inputs are finite; a program needn't handle non-finite values.
Results may differ from a plain program's by a relative error of at most 0.0001.
Values sent between devices are 32-bit elements; how exact they have to be, the bound alone decides.
No kernel may reach another device: no remote copies, remote signals or barrier semaphores. Data moves between devices by JAX's collectives and lax.ppermute only.
A program may use at most 128 MiB of HBM per device.

v0:
```python
import jax
import jax.numpy as jnp
from jax import lax
from jax.sharding import PartitionSpec as P

STEPS = 2
SWEEPS = 8


time_step = 0.02
molecular = 0.01
heat_diffuse = 0.01
eddy_coeff = 0.09
prod_coeff = 1.44
dissip_coeff = 1.92
turb_floor = 0.05
coupling = 1.0
thermal_gradient_factor = 0.3


def extended(block, sides, width):
    for axis, dim in sides:
        count = lax.axis_size(axis)
        forward = [(i, i + 1) for i in range(count - 1)]
        backward = [(target, source) for source, target in forward]
        low = lax.ppermute(
            lax.slice_in_dim(block, block.shape[dim] - width, None, axis=dim), axis, forward
        )
        high = lax.ppermute(lax.slice_in_dim(block, 0, width, axis=dim), axis, backward)
        block = jnp.concatenate([low, block, high], axis=dim)
    return block


def reduce_onto_parent(block):
    comps, depth, rows, cols = block.shape
    shaped = block.reshape(comps, depth // 2, 2, rows // 2, 2, cols // 2, 2)
    return jnp.mean(shaped, axis=(2, 4, 6))


def prolong(block):
    comps, depth, rows, cols = block.shape
    wide = jnp.broadcast_to(
        block[:, :, None, :, None, :, None], (comps, depth, 2, rows, 2, cols, 2)
    )
    return wide.reshape(comps, depth * 2, rows * 2, cols * 2)


def cross(left_vec, right_vec):
    return jnp.stack(
        [
            left_vec[1] * right_vec[2] - left_vec[2] * right_vec[1],
            left_vec[2] * right_vec[0] - left_vec[0] * right_vec[2],
            left_vec[0] * right_vec[1] - left_vec[1] * right_vec[0],
        ],
        0,
    )


def neighbours(padded):
    return (
        padded[:, 2:, 1:-1, 1:-1]
        + padded[:, :-2, 1:-1, 1:-1]
        + padded[:, 1:-1, 2:, 1:-1]
        + padded[:, 1:-1, :-2, 1:-1]
        + padded[:, 1:-1, 1:-1, 2:]
        + padded[:, 1:-1, 1:-1, :-2]
    )


def ohmic_admittance(zone_labels, zone_resistivity_inverse, heat_state):
    labels = jnp.arange(zone_resistivity_inverse.shape[0], dtype=jnp.int32)
    onehot = zone_labels[None] == labels[:, None, None, None]
    searched_higher = jnp.sum(
        jnp.where(onehot, zone_resistivity_inverse[:, None, None, None], jnp.float32(0.0)), axis=0
    )
    return (
        searched_higher
        * reduce_onto_parent(jnp.exp(-thermal_gradient_factor * heat_state)[None])[0]
    )


def faces(potential):
    padded = extended(potential, (("slab", 1),), 1)
    return jnp.pad(padded, ((0, 0), (0, 0), (1, 1), (1, 1)))


def relax(coupled, imposed_induction, winding_current, potential):
    conduct = coupled[3]
    motional = cross(coupled[:3], imposed_induction)
    source = conduct * motional + winding_current
    diagonal = 6.0 + coupling * conduct
    for sweep_index in range(SWEEPS):
        potential = (source + neighbours(faces(potential))) / diagonal
    drive_field = motional - coupling * potential
    current = conduct * drive_field + winding_current
    lorentz = cross(current, imposed_induction)
    joule = conduct * jnp.sum(drive_field * drive_field, axis=0)
    return (potential, jnp.concatenate([lorentz, joule[None]], 0))


def advance(padded, lorentz, joule):
    bordered = jnp.pad(padded, ((0, 0), (0, 0), (0, 0), (1, 1)))
    center = bordered[:, 1:-1, 1:-1, 1:-1]
    z_plus = bordered[:, 2:, 1:-1, 1:-1]
    z_minus = bordered[:, :-2, 1:-1, 1:-1]
    y_plus = bordered[:, 1:-1, 2:, 1:-1]
    y_minus = bordered[:, 1:-1, :-2, 1:-1]
    x_plus = bordered[:, 1:-1, 1:-1, 2:]
    x_minus = bordered[:, 1:-1, 1:-1, :-2]
    grad_z = 0.5 * (z_plus - z_minus)
    grad_y = 0.5 * (y_plus - y_minus)
    grad_x = 0.5 * (x_plus - x_minus)
    laplace = z_plus + z_minus + y_plus + y_minus + x_plus + x_minus - 6.0 * center
    kinetic = center[4]
    dissip = center[5]
    transport = center[0] * grad_x + center[1] * grad_y + center[2] * grad_z
    eddy_visc = eddy_coeff * kinetic * kinetic / jnp.maximum(dissip, turb_floor)
    strain = jnp.sum(
        grad_x[:3] * grad_x[:3] + grad_y[:3] * grad_y[:3] + grad_z[:3] * grad_z[:3], axis=0
    )
    produce = eddy_visc * strain
    diffuse = jnp.stack(
        [
            molecular + eddy_visc,
            molecular + eddy_visc,
            molecular + eddy_visc,
            heat_diffuse + eddy_visc / 0.9,
            molecular + eddy_visc,
            molecular + eddy_visc / 1.3,
        ],
        0,
    )
    dissip_source = (
        (prod_coeff * produce - dissip_coeff * dissip) * dissip / jnp.maximum(kinetic, turb_floor)
    )
    source = jnp.concatenate(
        [lorentz, joule[None], (produce - dissip)[None], dissip_source[None]], 0
    )
    return center + time_step * (diffuse * laplace - transport + source)


def flow_step(induction_tables, em_loads):
    padded = extended(induction_tables, (("slab", 1),), 1)
    padded = jnp.pad(padded, ((0, 0), (0, 0), (1, 1), (0, 0)))
    return advance(padded, em_loads[:3], em_loads[3])


def local_coupled(induction_tables, zone_labels, zone_resistivity_inverse):
    conduct = ohmic_admittance(zone_labels, zone_resistivity_inverse, induction_tables[3])
    return jnp.concatenate([reduce_onto_parent(induction_tables[:3]), conduct[None]], 0)


def on_device(
    melt_speeds,
    heat_state,
    eddy_quantities,
    zone_labels,
    zone_resistivity_inverse,
    imposed_induction,
    winding_current,
    window_entry_induction_guess,
):
    induction_tables = jnp.concatenate([melt_speeds, heat_state[None], eddy_quantities], 0)
    arrived = (
        lax.all_to_all(
            window_entry_induction_guess, "slab", split_axis=3, concat_axis=1, tiled=True
        ),
        lax.all_to_all(imposed_induction, "slab", split_axis=3, concat_axis=1, tiled=True),
        lax.all_to_all(winding_current, "slab", split_axis=3, concat_axis=1, tiled=True),
    )
    potential = jnp.transpose(arrived[0], (0, 3, 2, 1))
    field_local = jnp.transpose(arrived[1], (0, 3, 2, 1))
    coil_local = jnp.transpose(arrived[2], (0, 3, 2, 1))
    for step_index in range(STEPS):
        coupled = local_coupled(induction_tables, zone_labels, zone_resistivity_inverse)
        potential, em_loads = relax(coupled, field_local, coil_local, potential)
        induction_tables = flow_step(induction_tables, prolong(em_loads))
    potential = lax.all_to_all(
        jnp.transpose(potential, (0, 3, 2, 1)), "slab", split_axis=1, concat_axis=3, tiled=True
    )
    return (induction_tables[:3], induction_tables[3], induction_tables[4:], potential)


def solution(mesh):
    return jax.shard_map(
        on_device,
        mesh=mesh,
        in_specs=(
            P(None, ("groups", "slab"), None, None),
            P(("groups", "slab"), None, None),
            P(None, ("groups", "slab"), None, None),
            P(("groups", "slab"), None, None),
            P(),
            P(None, ("groups", "slab"), None, None),
            P(None, ("groups", "slab"), None, None),
            P(None, ("groups", "slab"), None, None),
        ),
        out_specs=(
            P(None, ("groups", "slab"), None, None),
            P(("groups", "slab"), None, None),
            P(None, ("groups", "slab"), None, None),
            P(None, ("groups", "slab"), None, None),
        ),
        check_vma=False,
    )
```

profile of v0, /device:TPU:0, one launch (start us, length us, event | category | flops | bytes accessed | tf_op | source)
XLA Modules:
  0.0 315.9 jit_solution(1965931268456075200)
XLA Ops:
  2.7 7.5 %all-to-all-start.2 = ((f32[16,1,768]{2,1,0:T(1,128)}), f32[16,1,768]{2,1,0:T(1,128)}, u32[]{:S(2)}, u32[]{:S(2)}) async-start(f32[16,1,768]{2,1,0:T(1,128)} %reshape.394), calls=%async_computation.2 | async-start | bytes 98304 | tf_op jit(solution)/shard_map/all_to_all | solution.py:165
  16.6 14.0 %reduce_sum.122 = f32[3,16,2,256,2]{4,3,2,1,0:T(8,128)} reshape(f32[3,32,512]{2,1,0:T(8,128)S(1)} %reduce_sum.121) | data formatting | bytes 393216 | tf_op jit(solution)/shard_map/reduce_sum | solution.py:37
  30.6 6.3 %reduce_sum.123 = f32[3,16,256]{2,1,0:T(8,128)S(1)} reduce(f32[3,16,2,256,2]{4,3,2,1,0:T(8,128)} %reduce_sum.122, f32[]{:T(128)} %constant.11.clone.1), dimensions={2,4}, to_apply=%region_4.5 | reduce | flops 36864 | bytes 245764 | tf_op jit(solution)/shard_map/reduce_sum | solution.py:37
  37.5 5.5 %reduce_sum.119 = f32[16,2,256,2]{3,2,1,0:T(8,128)} reshape(f32[32,512]{1,0:T(8,128)S(1)} %exponential_reduce_fusion) | data formatting | bytes 131072 | tf_op jit(solution)/shard_map/reduce_sum | solution.py:37
  48.7 6.9 %all-to-all-start = ((f32[16,1,768]{2,1,0:T(1,128)}), f32[16,1,768]{2,1,0:T(1,128)S(1)}, u32[]{:S(2)}, u32[]{:S(2)}) async-start(f32[16,1,768]{2,1,0:T(1,128)} %reshape.392), calls=%async_computation | async-start | bytes 98304 | tf_op jit(solution)/shard_map/all_to_all | solution.py:168
  62.7 7.0 %all-to-all-start.1 = ((f32[16,1,768]{2,1,0:T(1,128)}), f32[16,1,768]{2,1,0:T(1,128)}, u32[]{:S(2)}, u32[]{:S(2)}) async-start(f32[16,1,768]{2,1,0:T(1,128)} %reshape.390), calls=%async_computation.1 | async-start | bytes 98304 | tf_op jit(solution)/shard_map/all_to_all | solution.py:169
  71.2 5.4 %all-to-all-done.1 = f32[16,1,768]{2,1,0:T(1,128)} async-done(((f32[16,1,768]{2,1,0:T(1,128)}), f32[16,1,768]{2,1,0:T(1,128)}, u32[]{:S(2)}, u32[]{:S(2)}) %all-to-all-start.1) | async-done | bytes 49184 | tf_op jit(solution)/shard_map/all_to_all | solution.py:169
  99.7 5.6 %collective-permute-start.11 = (f32[3,1,16,256]{3,2,1,0:T(8,128)S(1)}, f32[3,1,16,256]{3,2,1,0:T(8,128)S(1)}, u32[]{:S(2)}, u32[]{:S(2)}) collective-permute-start(f32[3,1,16,256]{3,2,1,0:T(8,128)S(1)} %fusion.57), channel_id=1, source_target_pairs={{0,1},{1,2},{2,3},{3,4},{4,5},{5,6},{6,7},{7,8},{8,9},{9,10},{10,1... | collective-permute-start | bytes 147464 | tf_op jit(solution)/shard_map/ppermute | solution.py:26
  107.7 5.3 %collective-permute-start.13 = (f32[3,1,16,256]{3,2,1,0:T(8,128)S(1)}, f32[3,1,16,256]{3,2,1,0:T(8,128)S(1)}, u32[]{:S(2)}, u32[]{:S(2)}) collective-permute-start(f32[3,1,16,256]{3,2,1,0:T(8,128)S(1)} %fusion.55), channel_id=1, source_target_pairs={{0,1},{1,2},{2,3},{3,4},{4,5},{5,6},{6,7},{7,8},{8,9},{9,10},{10,1... | collective-permute-start | bytes 147464 | tf_op jit(solution)/shard_map/ppermute | solution.py:26
  115.5 5.4 %collective-permute-start.15 = (f32[3,1,16,256]{3,2,1,0:T(8,128)S(1)}, f32[3,1,16,256]{3,2,1,0:T(8,128)S(1)}, u32[]{:S(2)}, u32[]{:S(2)}) collective-permute-start(f32[3,1,16,256]{3,2,1,0:T(8,128)S(1)} %fusion.53), channel_id=1, source_target_pairs={{0,1},{1,2},{2,3},{3,4},{4,5},{5,6},{6,7},{7,8},{8,9},{9,10},{10,1... | collective-permute-start | bytes 147464 | tf_op jit(solution)/shard_map/ppermute | solution.py:26
  134.4 5.9 %collective-permute-start.21 = (f32[3,1,16,256]{3,2,1,0:T(8,128)}, f32[3,1,16,256]{3,2,1,0:T(8,128)}, u32[]{:S(2)}, u32[]{:S(2)}) collective-permute-start(f32[3,1,16,256]{3,2,1,0:T(8,128)} %get-tuple-element.31), channel_id=1, source_target_pairs={{0,1},{1,2},{2,3},{3,4},{4,5},{5,6},{6,7},{7,8},{8,9},{9,10},{10,1... | collective-permute-start | bytes 147464 | tf_op jit(solution)/shard_map/ppermute | solution.py:26
  146.4 9.8 %broadcast_in_dim.46 = f32[3,32,512]{2,1,0:T(8,128)S(1)} reshape(f32[3,16,2,256,2]{4,3,2,1,0:T(8,128)} %broadcast_in_dim.45) | data formatting | bytes 393216 | tf_op jit(solution)/shard_map/broadcast_in_dim | solution.py:42
  166.9 14.0 %reduce_sum.131 = f32[3,16,2,256,2]{4,3,2,1,0:T(8,128)} reshape(f32[3,32,512]{2,1,0:T(8,128)S(1)} %slice_reduce_fusion) | data formatting | bytes 393216 | tf_op jit(solution)/shard_map/reduce_sum | solution.py:37
  180.9 6.3 %reduce_sum.132 = f32[3,16,256]{2,1,0:T(8,128)S(1)} reduce(f32[3,16,2,256,2]{4,3,2,1,0:T(8,128)} %reduce_sum.131, f32[]{:T(128)} %constant.11.clone.1), dimensions={2,4}, to_apply=%region_10.11 | reduce | flops 36864 | bytes 245764 | tf_op jit(solution)/shard_map/reduce_sum | solution.py:37
  187.2 5.5 %reduce_sum.128 = f32[16,2,256,2]{3,2,1,0:T(8,128)} reshape(f32[32,512]{1,0:T(8,128)S(1)} %get-tuple-element.45) | data formatting | bytes 131072 | tf_op jit(solution)/shard_map/reduce_sum | solution.py:37
  206.5 5.8 %collective-permute-start.25 = (f32[3,1,16,256]{3,2,1,0:T(8,128)S(1)}, f32[3,1,16,256]{3,2,1,0:T(8,128)S(1)}, u32[]{:S(2)}, u32[]{:S(2)}) collective-permute-start(f32[3,1,16,256]{3,2,1,0:T(8,128)S(1)} %fusion.45), channel_id=1, source_target_pairs={{0,1},{1,2},{2,3},{3,4},{4,5},{5,6},{6,7},{7,8},{8,9},{9,10},{10,1... | collective-permute-start | bytes 147464 | tf_op jit(solution)/shard_map/ppermute | solution.py:26
  214.7 5.8 %collective-permute-start.27 = (f32[3,1,16,256]{3,2,1,0:T(8,128)S(1)}, f32[3,1,16,256]{3,2,1,0:T(8,128)S(1)}, u32[]{:S(2)}, u32[]{:S(2)}) collective-permute-start(f32[3,1,16,256]{3,2,1,0:T(8,128)S(1)} %fusion.43), channel_id=1, source_target_pairs={{0,1},{1,2},{2,3},{3,4},{4,5},{5,6},{6,7},{7,8},{8,9},{9,10},{10,1... | collective-permute-start | bytes 147464 | tf_op jit(solution)/shard_map/ppermute | solution.py:26
  222.9 5.5 %collective-permute-start.29 = (f32[3,1,16,256]{3,2,1,0:T(8,128)S(1)}, f32[3,1,16,256]{3,2,1,0:T(8,128)S(1)}, u32[]{:S(2)}, u32[]{:S(2)}) collective-permute-start(f32[3,1,16,256]{3,2,1,0:T(8,128)S(1)} %fusion.41), channel_id=1, source_target_pairs={{0,1},{1,2},{2,3},{3,4},{4,5},{5,6},{6,7},{7,8},{8,9},{9,10},{10,1... | collective-permute-start | bytes 147464 | tf_op jit(solution)/shard_map/ppermute | solution.py:26
  230.8 6.1 %collective-permute-start.31 = (f32[3,1,16,256]{3,2,1,0:T(8,128)S(1)}, f32[3,1,16,256]{3,2,1,0:T(8,128)S(1)}, u32[]{:S(2)}, u32[]{:S(2)}) collective-permute-start(f32[3,1,16,256]{3,2,1,0:T(8,128)S(1)} %fusion.39), channel_id=1, source_target_pairs={{0,1},{1,2},{2,3},{3,4},{4,5},{5,6},{6,7},{7,8},{8,9},{9,10},{10,1... | collective-permute-start | bytes 147464 | tf_op jit(solution)/shard_map/ppermute | solution.py:26
  238.2 5.8 %collective-permute-start.19 = (f32[6,1,32,512]{3,2,1,0:T(8,128)S(1)}, f32[6,1,32,512]{3,2,1,0:T(8,128)S(1)}, u32[]{:S(2)}, u32[]{:S(2)}) collective-permute-start(f32[6,1,32,512]{3,2,1,0:T(8,128)S(1)} %get-tuple-element.46), channel_id=1, source_target_pairs={{0,1},{1,2},{2,3},{3,4},{4,5},{5,6},{6,7},{7,8},{8,9},{9,10},{10,1... | collective-permute-start | bytes 1179656 | tf_op jit(solution)/shard_map/ppermute | solution.py:26
  245.6 6.0 %collective-permute-start.33 = (f32[3,1,16,256]{3,2,1,0:T(8,128)S(1)}, f32[3,1,16,256]{3,2,1,0:T(8,128)S(1)}, u32[]{:S(2)}, u32[]{:S(2)}) collective-permute-start(f32[3,1,16,256]{3,2,1,0:T(8,128)S(1)} %fusion.37), channel_id=1, source_target_pairs={{0,1},{1,2},{2,3},{3,4},{4,5},{5,6},{6,7},{7,8},{8,9},{9,10},{10,1... | collective-permute-start | bytes 147464 | tf_op jit(solution)/shard_map/ppermute | solution.py:26
  254.1 7.0 %collective-permute-start.35 = (f32[3,1,16,256]{3,2,1,0:T(8,128)S(1)}, f32[3,1,16,256]{3,2,1,0:T(8,128)S(1)}, u32[]{:S(2)}, u32[]{:S(2)}) collective-permute-start(f32[3,1,16,256]{3,2,1,0:T(8,128)S(1)} %fusion.35), channel_id=1, source_target_pairs={{0,1},{1,2},{2,3},{3,4},{4,5},{5,6},{6,7},{7,8},{8,9},{9,10},{10,1... | collective-permute-start | bytes 147464 | tf_op jit(solution)/shard_map/ppermute | solution.py:26
  270.2 10.3 %broadcast_in_dim.91 = f32[3,32,512]{2,1,0:T(8,128)} reshape(f32[3,16,2,256,2]{4,3,2,1,0:T(8,128)} %broadcast_in_dim.90) | data formatting | bytes 393216 | tf_op jit(solution)/shard_map/broadcast_in_dim | solution.py:42
  296.5 8.9 %all-to-all-start.3 = ((f32[16,1,768]{2,1,0:T(1,128)}), f32[16,1,768]{2,1,0:T(1,128)}, u32[]{:S(2)}, u32[]{:S(2)}) async-start(f32[16,1,768]{2,1,0:T(1,128)} %reshape.396), calls=%async_computation.3 | async-start | bytes 98304 | tf_op jit(solution)/shard_map/all_to_all | solution.py:178
  (270 shorter events, 142.1 us)
Async XLA Ops:
  2.7 46.1 %all-to-all-start.2 = ((f32[16,1,768]{2,1,0:T(1,128)}), f32[16,1,768]{2,1,0:T(1,128)}, u32[]{:S(2)}, u32[]{:S(2)}) async-start(f32[16,1,768]{2,1,0:T(1,128)} %reshape.394), calls=%async_computation.2 | async-start | bytes 98304 | tf_op jit(solution)/shard_map/all_to_all | solution.py:165
  11.4 109.4 %collective-permute-start = (f32[6,1,32,512]{3,2,1,0:T(8,128)S(1)}, f32[6,1,32,512]{3,2,1,0:T(8,128)S(1)}, u32[]{:S(2)}, u32[]{:S(2)}) collective-permute-start(f32[6,1,32,512]{3,2,1,0:T(8,128)S(1)} %get-tuple-element.49), channel_id=1, source_target_pairs={{1,0},{2,1},{3,2},{4,3},{5,4},{6,5},{7,6},{8,7},{9,8},{10,9},{11,1... | collective-permute-start | bytes 1179656 | tf_op jit(solution)/shard_map/ppermute | solution.py:29
  12.7 108.1 %collective-permute-start.1 = (f32[6,1,32,512]{3,2,1,0:T(8,128)S(1)}, f32[6,1,32,512]{3,2,1,0:T(8,128)S(1)}, u32[]{:S(2)}, u32[]{:S(2)}) collective-permute-start(f32[6,1,32,512]{3,2,1,0:T(8,128)S(1)} %get-tuple-element.48), channel_id=1, source_target_pairs={{0,1},{1,2},{2,3},{3,4},{4,5},{5,6},{6,7},{7,8},{8,9},{9,10},{10,1... | collective-permute-start | bytes 1179656 | tf_op jit(solution)/shard_map/ppermute | solution.py:26
  48.7 14.0 %all-to-all-start = ((f32[16,1,768]{2,1,0:T(1,128)}), f32[16,1,768]{2,1,0:T(1,128)S(1)}, u32[]{:S(2)}, u32[]{:S(2)}) async-start(f32[16,1,768]{2,1,0:T(1,128)} %reshape.392), calls=%async_computation | async-start | bytes 98304 | tf_op jit(solution)/shard_map/all_to_all | solution.py:168
  58.4 20.4 %collective-permute-start.2 = (f32[3,1,16,256]{3,2,1,0:T(8,128)S(1)}, f32[3,1,16,256]{3,2,1,0:T(8,128)S(1)}, u32[]{:S(2)}, u32[]{:S(2)}) collective-permute-start(f32[3,1,16,256]{3,2,1,0:T(8,128)S(1)} %bitcast.204), channel_id=1, source_target_pairs={{1,0},{2,1},{3,2},{4,3},{5,4},{6,5},{7,6},{8,7},{9,8},{10,9},{11,1... | collective-permute-start | bytes 147464 | tf_op jit(solution)/shard_map/ppermute | solution.py:29
  59.7 19.1 %collective-permute-start.3 = (f32[3,1,16,256]{3,2,1,0:T(8,128)S(1)}, f32[3,1,16,256]{3,2,1,0:T(8,128)S(1)}, u32[]{:S(2)}, u32[]{:S(2)}) collective-permute-start(f32[3,1,16,256]{3,2,1,0:T(8,128)S(1)} %bitcast.205), channel_id=1, source_target_pairs={{0,1},{1,2},{2,3},{3,4},{4,5},{5,6},{6,7},{7,8},{8,9},{9,10},{10,1... | collective-permute-start | bytes 147464 | tf_op jit(solution)/shard_map/ppermute | solution.py:26
  62.7 13.9 %all-to-all-start.1 = ((f32[16,1,768]{2,1,0:T(1,128)}), f32[16,1,768]{2,1,0:T(1,128)}, u32[]{:S(2)}, u32[]{:S(2)}) async-start(f32[16,1,768]{2,1,0:T(1,128)} %reshape.390), calls=%async_computation.1 | async-start | bytes 98304 | tf_op jit(solution)/shard_map/all_to_all | solution.py:169
  98.4 6.9 %collective-permute-start.10 = (f32[3,1,16,256]{3,2,1,0:T(8,128)S(1)}, f32[3,1,16,256]{3,2,1,0:T(8,128)S(1)}, u32[]{:S(2)}, u32[]{:S(2)}) collective-permute-start(f32[3,1,16,256]{3,2,1,0:T(8,128)S(1)} %fusion.57), channel_id=1, source_target_pairs={{1,0},{2,1},{3,2},{4,3},{5,4},{6,5},{7,6},{8,7},{9,8},{10,9},{11,1... | collective-permute-start | bytes 147464 | tf_op jit(solution)/shard_map/ppermute | solution.py:29
  114.2 10.7 %collective-permute-start.14 = (f32[3,1,16,256]{3,2,1,0:T(8,128)S(1)}, f32[3,1,16,256]{3,2,1,0:T(8,128)S(1)}, u32[]{:S(2)}, u32[]{:S(2)}) collective-permute-start(f32[3,1,16,256]{3,2,1,0:T(8,128)S(1)} %fusion.53), channel_id=1, source_target_pairs={{1,0},{2,1},{3,2},{4,3},{5,4},{6,5},{7,6},{8,7},{9,8},{10,9},{11,1... | collective-permute-start | bytes 147464 | tf_op jit(solution)/shard_map/ppermute | solution.py:29
  115.5 9.4 %collective-permute-start.15 = (f32[3,1,16,256]{3,2,1,0:T(8,128)S(1)}, f32[3,1,16,256]{3,2,1,0:T(8,128)S(1)}, u32[]{:S(2)}, u32[]{:S(2)}) collective-permute-start(f32[3,1,16,256]{3,2,1,0:T(8,128)S(1)} %fusion.53), channel_id=1, source_target_pairs={{0,1},{1,2},{2,3},{3,4},{4,5},{5,6},{6,7},{7,8},{8,9},{9,10},{10,1... | collective-permute-start | bytes 147464 | tf_op jit(solution)/shard_map/ppermute | solution.py:26
  125.1 6.9 %collective-permute-start.16 = (f32[3,1,16,256]{3,2,1,0:T(8,128)S(1)}, f32[3,1,16,256]{3,2,1,0:T(8,128)S(1)}, u32[]{:S(2)}, u32[]{:S(2)}) collective-permute-start(f32[3,1,16,256]{3,2,1,0:T(8,128)S(1)} %fusion.51), channel_id=1, source_target_pairs={{1,0},{2,1},{3,2},{4,3},{5,4},{6,5},{7,6},{8,7},{9,8},{10,9},{11,1... | collective-permute-start | bytes 147464 | tf_op jit(solution)/shard_map/ppermute | solution.py:29
  133.1 62.5 %collective-permute-start.20 = (f32[3,1,16,256]{3,2,1,0:T(8,128)}, f32[3,1,16,256]{3,2,1,0:T(8,128)}, u32[]{:S(2)}, u32[]{:S(2)}) collective-permute-start(f32[3,1,16,256]{3,2,1,0:T(8,128)} %get-tuple-element.31), channel_id=1, source_target_pairs={{1,0},{2,1},{3,2},{4,3},{5,4},{6,5},{7,6},{8,7},{9,8},{10,9},{11,1... | collective-permute-start | bytes 147464 | tf_op jit(solution)/shard_map/ppermute | solution.py:29
  134.4 61.3 %collective-permute-start.21 = (f32[3,1,16,256]{3,2,1,0:T(8,128)}, f32[3,1,16,256]{3,2,1,0:T(8,128)}, u32[]{:S(2)}, u32[]{:S(2)}) collective-permute-start(f32[3,1,16,256]{3,2,1,0:T(8,128)} %get-tuple-element.31), channel_id=1, source_target_pairs={{0,1},{1,2},{2,3},{3,4},{4,5},{5,6},{6,7},{7,8},{8,9},{9,10},{10,1... | collective-permute-start | bytes 147464 | tf_op jit(solution)/shard_map/ppermute | solution.py:26
  205.2 7.1 %collective-permute-start.24 = (f32[3,1,16,256]{3,2,1,0:T(8,128)S(1)}, f32[3,1,16,256]{3,2,1,0:T(8,128)S(1)}, u32[]{:S(2)}, u32[]{:S(2)}) collective-permute-start(f32[3,1,16,256]{3,2,1,0:T(8,128)S(1)} %fusion.45), channel_id=1, source_target_pairs={{1,0},{2,1},{3,2},{4,3},{5,4},{6,5},{7,6},{8,7},{9,8},{10,9},{11,1... | collective-permute-start | bytes 147464 | tf_op jit(solution)/shard_map/ppermute | solution.py:29
  213.4 7.1 %collective-permute-start.26 = (f32[3,1,16,256]{3,2,1,0:T(8,128)S(1)}, f32[3,1,16,256]{3,2,1,0:T(8,128)S(1)}, u32[]{:S(2)}, u32[]{:S(2)}) collective-permute-start(f32[3,1,16,256]{3,2,1,0:T(8,128)S(1)} %fusion.43), channel_id=1, source_target_pairs={{1,0},{2,1},{3,2},{4,3},{5,4},{6,5},{7,6},{8,7},{9,8},{10,9},{11,1... | collective-permute-start | bytes 147464 | tf_op jit(solution)/shard_map/ppermute | solution.py:29
  229.5 14.5 %collective-permute-start.30 = (f32[3,1,16,256]{3,2,1,0:T(8,128)S(1)}, f32[3,1,16,256]{3,2,1,0:T(8,128)S(1)}, u32[]{:S(2)}, u32[]{:S(2)}) collective-permute-start(f32[3,1,16,256]{3,2,1,0:T(8,128)S(1)} %fusion.39), channel_id=1, source_target_pairs={{1,0},{2,1},{3,2},{4,3},{5,4},{6,5},{7,6},{8,7},{9,8},{10,9},{11,1... | collective-permute-start | bytes 147464 | tf_op jit(solution)/shard_map/ppermute | solution.py:29
  230.8 13.2 %collective-permute-start.31 = (f32[3,1,16,256]{3,2,1,0:T(8,128)S(1)}, f32[3,1,16,256]{3,2,1,0:T(8,128)S(1)}, u32[]{:S(2)}, u32[]{:S(2)}) collective-permute-start(f32[3,1,16,256]{3,2,1,0:T(8,128)S(1)} %fusion.39), channel_id=1, source_target_pairs={{0,1},{1,2},{2,3},{3,4},{4,5},{5,6},{6,7},{7,8},{8,9},{9,10},{10,1... | collective-permute-start | bytes 147464 | tf_op jit(solution)/shard_map/ppermute | solution.py:26
  236.9 24.2 %collective-permute-start.18 = (f32[6,1,32,512]{3,2,1,0:T(8,128)S(1)}, f32[6,1,32,512]{3,2,1,0:T(8,128)S(1)}, u32[]{:S(2)}, u32[]{:S(2)}) collective-permute-start(f32[6,1,32,512]{3,2,1,0:T(8,128)S(1)} %get-tuple-element.47), channel_id=1, source_target_pairs={{1,0},{2,1},{3,2},{4,3},{5,4},{6,5},{7,6},{8,7},{9,8},{10,9},{11,1... | collective-permute-start | bytes 1179656 | tf_op jit(solution)/shard_map/ppermute | solution.py:29
  238.2 22.9 %collective-permute-start.19 = (f32[6,1,32,512]{3,2,1,0:T(8,128)S(1)}, f32[6,1,32,512]{3,2,1,0:T(8,128)S(1)}, u32[]{:S(2)}, u32[]{:S(2)}) collective-permute-start(f32[6,1,32,512]{3,2,1,0:T(8,128)S(1)} %get-tuple-element.46), channel_id=1, source_target_pairs={{0,1},{1,2},{2,3},{3,4},{4,5},{5,6},{6,7},{7,8},{8,9},{9,10},{10,1... | collective-permute-start | bytes 1179656 | tf_op jit(solution)/shard_map/ppermute | solution.py:26
  244.3 7.4 %collective-permute-start.32 = (f32[3,1,16,256]{3,2,1,0:T(8,128)S(1)}, f32[3,1,16,256]{3,2,1,0:T(8,128)S(1)}, u32[]{:S(2)}, u32[]{:S(2)}) collective-permute-start(f32[3,1,16,256]{3,2,1,0:T(8,128)S(1)} %fusion.37), channel_id=1, source_target_pairs={{1,0},{2,1},{3,2},{4,3},{5,4},{6,5},{7,6},{8,7},{9,8},{10,9},{11,1... | collective-permute-start | bytes 147464 | tf_op jit(solution)/shard_map/ppermute | solution.py:29
  245.6 6.9 %collective-permute-start.33 = (f32[3,1,16,256]{3,2,1,0:T(8,128)S(1)}, f32[3,1,16,256]{3,2,1,0:T(8,128)S(1)}, u32[]{:S(2)}, u32[]{:S(2)}) collective-permute-start(f32[3,1,16,256]{3,2,1,0:T(8,128)S(1)} %fusion.37), channel_id=1, source_target_pairs={{0,1},{1,2},{2,3},{3,4},{4,5},{5,6},{6,7},{7,8},{8,9},{9,10},{10,1... | collective-permute-start | bytes 147464 | tf_op jit(solution)/shard_map/ppermute | solution.py:26
  252.8 11.2 %collective-permute-start.34 = (f32[3,1,16,256]{3,2,1,0:T(8,128)S(1)}, f32[3,1,16,256]{3,2,1,0:T(8,128)S(1)}, u32[]{:S(2)}, u32[]{:S(2)}) collective-permute-start(f32[3,1,16,256]{3,2,1,0:T(8,128)S(1)} %fusion.35), channel_id=1, source_target_pairs={{1,0},{2,1},{3,2},{4,3},{5,4},{6,5},{7,6},{8,7},{9,8},{10,9},{11,1... | collective-permute-start | bytes 147464 | tf_op jit(solution)/shard_map/ppermute | solution.py:29
  254.1 9.9 %collective-permute-start.35 = (f32[3,1,16,256]{3,2,1,0:T(8,128)S(1)}, f32[3,1,16,256]{3,2,1,0:T(8,128)S(1)}, u32[]{:S(2)}, u32[]{:S(2)}) collective-permute-start(f32[3,1,16,256]{3,2,1,0:T(8,128)S(1)} %fusion.35), channel_id=1, source_target_pairs={{0,1},{1,2},{2,3},{3,4},{4,5},{5,6},{6,7},{7,8},{8,9},{9,10},{10,1... | collective-permute-start | bytes 147464 | tf_op jit(solution)/shard_map/ppermute | solution.py:26
  296.5 15.8 %all-to-all-start.3 = ((f32[16,1,768]{2,1,0:T(1,128)}), f32[16,1,768]{2,1,0:T(1,128)}, u32[]{:S(2)}, u32[]{:S(2)}) async-start(f32[16,1,768]{2,1,0:T(1,128)} %reshape.396), calls=%async_computation.3 | async-start | bytes 98304 | tf_op jit(solution)/shard_map/all_to_all | solution.py:178
  (59 other events, 543.3 us)
where the time goes:
time: 318 us; the launch traced here: 316 us
  starting transfers between devices  146 us (46%)
  local copies, waits for them, and re-layouts  102 us (32%)
  other arithmetic  52.2 us (16%)
  waiting for transfers between devices  13.8 us (4%)
    ppermute x18, starting transfers between devices, extended(): lax.ppermute(lax.slice_in_dim(block, block.shape[dim] - width, None, axis...  91.7 us
    broadcast_in_dim x12, local copies, waits for them, and re-layouts, prolong(): jnp.broadcast_to(block[:, :, None, :, None, :, None], (comps, depth, 2, r...  46.2 us
    reduce_sum x4, local copies, waits for them, and re-layouts, reduce_onto_parent(): return jnp.mean(shaped, axis=(2, 4, 6))  39 us
    ppermute x18, starting transfers between devices, extended(): lax.ppermute(lax.slice_in_dim(block, 0, width, axis=dim), axis, backward)  23.5 us
    reduce_sum x7, other arithmetic, reduce_onto_parent(): return jnp.mean(shaped, axis=(2, 4, 6))  18.3 us
    unnamed x98, local copies, waits for them, and re-layouts  10.5 us
    all_to_all x1, starting transfers between devices, on_device(): lax.all_to_all(jnp.transpose(potential, (0, 3, 2, 1)), 'slab', split_axis...  8.93 us
    ppermute x18, waiting for transfers between devices, extended(): lax.ppermute(lax.slice_in_dim(block, block.shape[dim] - width, None, axis...  8.3 us
  transfers between devices with their start and end apart: 40, of which 12 were waited for; matrix products, arithmetic and copies ran while one was open for 35% of the time, Pallas kernels for 0%

commit v1 on v0

--- a/solution.py
+++ b/solution.py
@@ -1,6 +1,10 @@
+import functools
+
 import jax
 import jax.numpy as jnp
 from jax import lax
+from jax.experimental import pallas as pl
+from jax.experimental.pallas import tpu as pltpu
 from jax.sharding import PartitionSpec as P
 
 STEPS = 2
@@ -150,7 +154,7 @@
     return jnp.concatenate([reduce_onto_parent(induction_tables[:3]), conduct[None]], 0)
 
 
-def on_device(
+def per_sweep_plan(
     melt_speeds,
     heat_state,
     eddy_quantities,
@@ -181,6 +185,458 @@
     return (induction_tables[:3], induction_tables[3], induction_tables[4:], potential)
 
 
+HALO = 2 * SWEEPS
+LANES = 128
+
+
+def exact_dot(values, chooser):
+    high = values.astype(jnp.bfloat16)
+    rest = values - high.astype(jnp.float32)
+    middle = rest.astype(jnp.bfloat16)
+    low = (rest - middle.astype(jnp.float32)).astype(jnp.bfloat16)
+    rows = values.shape[0]
+    parts = jnp.dot(
+        jnp.concatenate([high, middle, low], 0), chooser, preferred_element_type=jnp.float32
+    )
+    return parts[:rows] + (parts[rows : 2 * rows] + parts[2 * rows :])
+
+
+def pair_chooser(wide, weight, transposed):
+    shape = (wide // 2, wide) if transposed else (wide, wide // 2)
+    fine = lax.broadcasted_iota(jnp.int32, shape, 1 if transposed else 0)
+    coarse = lax.broadcasted_iota(jnp.int32, shape, 0 if transposed else 1)
+    picked = lax.shift_right_logical(fine, 1) == coarse
+    return jnp.where(picked, jnp.float32(weight), jnp.float32(0.0)).astype(jnp.bfloat16)
+
+
+def pack_windows(sums_ref, labels_ref, table_ref, send_ref, halo):
+    tiles, rows, _ = sums_ref.shape
+    wide = tiles * LANES
+    count, ny = send_ref.shape[0], labels_ref.shape[1]
+    paired = jnp.concatenate(
+        [
+            sums_ref[t, pl.ds(0, rows // 2, stride=2), :] + sums_ref[t, pl.ds(1, rows // 2, stride=2), :]
+            for t in range(tiles)
+        ],
+        1,
+    )
+    coarse = exact_dot(paired, pair_chooser(wide, 0.125, False))
+    labels = labels_ref[0]
+    admittance = jnp.zeros(labels.shape, jnp.float32)
+    for region in range(table_ref.shape[0]):
+        admittance = jnp.where(labels == region, table_ref[region], admittance)
+    coupled = jnp.concatenate([coarse[: 3 * ny], coarse[3 * ny :] * admittance], 0)
+    nx = wide // 2
+    chunk = nx // count
+    window = chunk + 2 * halo
+    padded = jnp.concatenate([coupled, jnp.zeros((4 * ny, LANES), jnp.float32)], 1)
+    padded = pltpu.roll(padded, halo, 1)
+    for target in range(count):
+        start = target * chunk
+        joined = jnp.concatenate(
+            [padded[f * ny : (f + 1) * ny, start : start + window] for f in range(4)], 1
+        )
+        send_ref[target, :ny, :] = joined[:, :LANES]
+        if 4 * window > LANES:
+            half = ny // 2
+            send_ref[target, ny:, :] = jnp.concatenate(
+                [joined[:half, LANES:], joined[half:, LANES:]], 1
+            )
+
+
+def open_kernel(
+    vel_ref,
+    heat_ref,
+    turb_ref,
+    labels_ref,
+    table_ref,
+    guess_ref,
+    applied_ref,
+    coil_ref,
+    send_ref,
+    block_ref,
+    mate_ref,
+    cross_ref,
+    sums_ref,
+    flat_ref,
+):
+    odd = lax.rem(lax.axis_index("slab"), 2)
+    planes = [(vel_ref, 0), (vel_ref, 1), (vel_ref, 2), (heat_ref, None), (turb_ref, 0), (turb_ref, 1)]
+    for f, (ref, comp) in enumerate(planes):
+        if comp is None:
+            mate_ref[f] = ref[1 - odd]
+            cross_ref[f] = ref[odd]
+        else:
+            mate_ref[f] = ref[comp, 1 - odd]
+            cross_ref[f] = ref[comp, odd]
+    rows = heat_ref.shape[1]
+    for t in range(sums_ref.shape[0]):
+        at = slice(t * LANES, (t + 1) * LANES)
+        for c in range(3):
+            sums_ref[t, c * rows : (c + 1) * rows, :] = vel_ref[c, 0, :, at] + vel_ref[c, 1, :, at]
+        sums_ref[t, 3 * rows :, :] = jnp.exp(
+            -thermal_gradient_factor * heat_ref[0, :, at]
+        ) + jnp.exp(-thermal_gradient_factor * heat_ref[1, :, at])
+    total, nz = guess_ref.shape
+    ny = labels_ref.shape[1]
+    stacked = total // ny
+    for kind, ref in enumerate((guess_ref, applied_ref, coil_ref)):
+        flat_ref[:, kind * nz : (kind + 1) * nz] = ref[...]
+    lines = [flat_ref[pl.ds(y, stacked, stride=ny), :] for y in range(ny)]
+    for kind in range(3):
+        block_ref[kind * stacked : (kind + 1) * stacked, :] = jnp.concatenate(
+            [line[:, kind * nz : (kind + 1) * nz] for line in lines], 1
+        )
+    pack_windows(sums_ref, labels_ref, table_ref, send_ref, HALO)
+
+
+def solve_kernel(chunk, ny, nz, first, *refs):
+    if first:
+        recv_ref, block_ref, mate_ref, cross_ref, pot_out, send_ref, wide_ref, turn_ref = refs
+        halo = HALO
+    else:
+        recv_ref, block_ref, mate_ref, cross_ref, pot_in, pot_out, send_ref = refs[:7]
+        wide_ref, turn_ref, flat_ref = refs[7:]
+        halo = HALO - SWEEPS
+    window = chunk + 2 * halo
+    place = lax.axis_index("slab")
+    count = lax.axis_size("slab")
+    odd = lax.rem(place, 2)
+    half = ny // 2
+    for z in range(nz):
+        wide_ref[0, pl.ds(z, ny, stride=nz), :] = recv_ref[z, :ny, :]
+        if 4 * window > LANES:
+            tail = recv_ref[z, ny:, :]
+            wide_ref[1, pl.ds(z, half, stride=nz), :] = tail
+            wide_ref[1, pl.ds(half * nz + z, half, stride=nz), :] = pltpu.roll(tail, LANES // 2, 1)
+    turned = jnp.concatenate([jnp.transpose(wide_ref[t]) for t in range(wide_ref.shape[0])], 0)
+    velocity = [turned[c * window : (c + 1) * window] for c in range(3)]
+    conduct = turned[3 * window : 4 * window]
+
+    def windowed(kind):
+        found = []
+        for c in range(3):
+            base = (kind * 3 + c) * chunk
+            mate, cross_side = mate_ref[base : base + chunk, :], cross_ref[base : base + chunk, :]
+            low = jnp.where(odd == 0, cross_side, mate)
+            high = jnp.where(odd == 0, mate, cross_side)
+            found.append(
+                jnp.concatenate(
+                    [low[chunk - halo :], block_ref[base : base + chunk, :], high[:halo]], 0
+                )
+            )
+        return found
+
+    applied, coil = windowed(1), windowed(2)
+    potential = jnp.concatenate(windowed(0), 0) if first else pot_in[...]
+    motional = [
+        velocity[1] * applied[2] - velocity[2] * applied[1],
+        velocity[2] * applied[0] - velocity[0] * applied[2],
+        velocity[0] * applied[1] - velocity[1] * applied[0],
+    ]
+    where_x = place * chunk - halo + lax.broadcasted_iota(jnp.int32, (window, ny * nz), 0)
+    inside = (where_x >= 0) & (where_x < count * chunk)
+    inverse = jnp.where(inside, 1.0 / (6.0 + coupling * conduct), 0.0)
+    source = jnp.concatenate([conduct * motional[c] + coil[c] for c in range(3)], 0)
+    inverse = jnp.concatenate([inverse] * 3, 0)
+    source = source * inverse
+    shape = potential.shape
+    lane = lax.broadcasted_iota(jnp.int32, shape, 1)
+    column = lax.rem(lane, nz)
+    for sweep in range(SWEEPS):
+        around = pltpu.roll(potential, 1, 0) + pltpu.roll(potential, shape[0] - 1, 0)
+        around += jnp.where(column == 0, 0.0, pltpu.roll(potential, 1, 1))
+        around += jnp.where(column == nz - 1, 0.0, pltpu.roll(potential, shape[1] - 1, 1))
+        around += jnp.where(lane < nz, 0.0, pltpu.roll(potential, nz, 1))
+        around += jnp.where(lane >= shape[1] - nz, 0.0, pltpu.roll(potential, shape[1] - nz, 1))
+        potential = source + around * inverse
+    own = [potential[c * window + halo : c * window + halo + chunk] for c in range(3)]
+    if first:
+        keep = chunk + 2 * (halo - SWEEPS)
+        for c in range(3):
+            pot_out[c * keep : (c + 1) * keep, :] = potential[
+                c * window + SWEEPS : c * window + SWEEPS + keep
+            ]
+    else:
+        together = jnp.concatenate(own, 0)
+        lanes = ny * nz
+        for y in range(ny):
+            line = pltpu.roll(together, lanes - y * nz, 1) if y else together
+            flat_ref[pl.ds(y, 3 * chunk, stride=ny), :] = line[:, :LANES]
+        pot_out[...] = flat_ref[:, :nz]
+    mine = slice(halo, halo + chunk)
+    conduct_own = conduct[mine]
+    applied_own = [a[mine] for a in applied]
+    drive = [motional[c][mine] - coupling * own[c] for c in range(3)]
+    current = [conduct_own * drive[c] + coil[c][mine] for c in range(3)]
+    loads = [
+        current[1] * applied_own[2] - current[2] * applied_own[1],
+        current[2] * applied_own[0] - current[0] * applied_own[2],
+        current[0] * applied_own[1] - current[1] * applied_own[0],
+        conduct_own * (drive[0] * drive[0] + drive[1] * drive[1] + drive[2] * drive[2]),
+    ]
+    loads = jnp.concatenate(loads, 0)
+    middle = half * nz
+    turn_ref[...] = jnp.transpose(jnp.concatenate([loads[:, :middle], loads[:, middle:]], 0))
+    for z in range(nz):
+        send_ref[z] = turn_ref[pl.ds(z, half, stride=nz), :]
+
+
+def flow_kernel(last, *refs):
+    vel_ref, heat_ref, turb_ref, mate_ref, cross_ref, recv_ref = refs[:6]
+    if last:
+        vel_out, heat_out, turb_out, bordered_ref, loads_ref = refs[6:]
+    else:
+        labels_ref, table_ref = refs[6:8]
+        vel_out, heat_out, turb_out, send_ref, mate_out, cross_out = refs[8:14]
+        bordered_ref, loads_ref, sums_ref = refs[14:]
+    odd = lax.rem(lax.axis_index("slab"), 2)
+    rows, wide = heat_ref.shape[1:]
+    count, half, packed = recv_ref.shape
+    chunk = packed // 8
+    edge = jnp.zeros((8, wide), jnp.float32)
+    for f in range(6):
+        for plane in range(2):
+            bordered_ref[f, plane, 0:8, :] = edge
+            bordered_ref[f, plane, 8 + rows :, :] = edge
+            if f < 3:
+                block = vel_ref[f, plane]
+            elif f == 3:
+                block = heat_ref[plane]
+            else:
+                block = turb_ref[f - 4, plane]
+            bordered_ref[f, plane, 8 : 8 + rows, :] = block
+    stacked = []
+    for f in range(4):
+        for side in range(2):
+            at = (side * 4 + f) * chunk
+            stacked.append(
+                jnp.concatenate([recv_ref[s, :, at : at + chunk] for s in range(count)], 1)
+            )
+    spread = exact_dot(jnp.concatenate(stacked, 0), pair_chooser(wide, 1.0, True))
+    for t in range(wide // LANES):
+        part = spread[:, t * LANES : (t + 1) * LANES]
+        loads_ref[t, pl.ds(0, 2 * rows, stride=2), :] = part
+        loads_ref[t, pl.ds(1, 2 * rows, stride=2), :] = part
+    lane = lax.broadcasted_iota(jnp.int32, (8, wide), 1)
+    first_lane, last_lane = lane == 0, lane == wide - 1
+    for top in range(0, rows, 8):
+        tile = slice(top, top + 8)
+        for plane in range(2):
+            center = [bordered_ref[f, plane, 8 + top : 16 + top, :] for f in range(6)]
+            kinetic, dissip = center[4], center[5]
+            eddy_visc = eddy_coeff * kinetic * kinetic / jnp.maximum(dissip, turb_floor)
+            strain = jnp.zeros((8, wide), jnp.float32)
+            for f in range(6):
+                here = center[f]
+                mate, cross_side = mate_ref[f, tile, :], cross_ref[f, tile, :]
+                other = bordered_ref[f, 1 - plane, 8 + top : 16 + top, :]
+                if plane == 0:
+                    z_minus, z_plus = jnp.where(odd == 0, cross_side, mate), other
+                else:
+                    z_minus, z_plus = other, jnp.where(odd == 0, mate, cross_side)
+                y_minus = bordered_ref[f, plane, 7 + top : 15 + top, :]
+                y_plus = bordered_ref[f, plane, 9 + top : 17 + top, :]
+                x_minus = jnp.where(first_lane, 0.0, pltpu.roll(here, 1, 1))
+                x_plus = jnp.where(last_lane, 0.0, pltpu.roll(here, wide - 1, 1))
+                grad_z = 0.5 * (z_plus - z_minus)
+                grad_y = 0.5 * (y_plus - y_minus)
+                grad_x = 0.5 * (x_plus - x_minus)
+                laplace = z_plus + z_minus + y_plus + y_minus + x_plus + x_minus - 6.0 * here
+                transport = center[0] * grad_x + center[1] * grad_y + center[2] * grad_z
+                if f < 3:
+                    strain += grad_x * grad_x + grad_y * grad_y + grad_z * grad_z
+                    diffuse = molecular + eddy_visc
+                    source = jnp.concatenate(
+                        [
+                            loads_ref[t, f * rows + top : f * rows + top + 8, :]
+                            for t in range(wide // LANES)
+                        ],
+                        1,
+                    )
+                elif f == 3:
+                    diffuse = heat_diffuse + eddy_visc * (1.0 / 0.9)
+                    source = jnp.concatenate(
+                        [
+                            loads_ref[t, f * rows + top : f * rows + top + 8, :]
+                            for t in range(wide // LANES)
+                        ],
+                        1,
+                    )
+                elif f == 4:
+                    produce = eddy_visc * strain
+                    diffuse = molecular + eddy_visc
+                    source = produce - dissip
+                else:
+                    diffuse = molecular + eddy_visc * (1.0 / 1.3)
+                    source = (
+                        (prod_coeff * produce - dissip_coeff * dissip)
+                        * dissip
+                        / jnp.maximum(kinetic, turb_floor)
+                    )
+                fresh = here + time_step * (diffuse * laplace - transport + source)
+                if f < 3:
+                    vel_out[f, plane, tile, :] = fresh
+                elif f == 3:
+                    heat_out[plane, tile, :] = fresh
+                else:
+                    turb_out[f - 4, plane, tile, :] = fresh
+                if not last and f < 4:
+                    part = jnp.exp(-thermal_gradient_factor * fresh) if f == 3 else fresh
+                    spot = slice(f * rows + top, f * rows + top + 8)
+                    for t in range(wide // LANES):
+                        piece = part[:, t * LANES : (t + 1) * LANES]
+                        sums_ref[t, spot, :] = piece if plane == 0 else sums_ref[t, spot, :] + piece
+    if last:
+        return
+    outs = [(vel_out, 0), (vel_out, 1), (vel_out, 2), (heat_out, None), (turb_out, 0), (turb_out, 1)]
+    for f, (ref, comp) in enumerate(outs):
+        if comp is None:
+            mate_out[f] = ref[1 - odd]
+            cross_out[f] = ref[odd]
+        else:
+            mate_out[f] = ref[comp, 1 - odd]
+            cross_out[f] = ref[comp, odd]
+    pack_windows(sums_ref, labels_ref, table_ref, send_ref, HALO - SWEEPS)
+
+
+def call(kernel, outs, scratch, name, table_at, cost, *operands):
+    vmem = pl.BlockSpec(memory_space=pltpu.VMEM)
+    smem = pl.BlockSpec(memory_space=pltpu.SMEM)
+    return pl.pallas_call(
+        kernel,
+        out_shape=[jax.ShapeDtypeStruct(s, jnp.float32) for s in outs],
+        in_specs=[smem if i == table_at else vmem for i in range(len(operands))],
+        out_specs=[vmem] * len(outs),
+        scratch_shapes=[pltpu.VMEM(s, jnp.float32) for s in scratch],
+        name=name,
+        cost_estimate=pl.CostEstimate(flops=cost, bytes_accessed=4 * cost // 64, transcendentals=0),
+    )(*operands)
+
+
+def beside(block):
+    count = lax.axis_size("slab")
+    mates = [(i, i ^ 1) for i in range(count)]
+    across = [(i, i + 1) for i in range(1, count - 1, 2)]
+    across = across + [(b, a) for a, b in across]
+    return mates, across
+
+
+def window_plan(
+    melt_speeds,
+    heat_state,
+    eddy_quantities,
+    zone_labels,
+    zone_resistivity_inverse,
+    imposed_induction,
+    winding_current,
+    window_entry_induction_guess,
+):
+    count = lax.axis_size("slab")
+    _, chunk, ny, nz = imposed_induction.shape
+    _, rows, wide = heat_state.shape
+    mates, across = beside(None)
+    flat = [
+        a.reshape(3 * chunk * ny, nz)
+        for a in (window_entry_induction_guess, imposed_induction, winding_current)
+    ]
+    window, narrow = chunk + 2 * HALO, chunk + 2 * (HALO - SWEEPS)
+    tall = ny + ny // 2 if 4 * window > LANES else ny
+    plane = (6, rows, wide)
+    sums = (wide // LANES, 4 * rows, LANES)
+    fields = (melt_speeds, heat_state, eddy_quantities)
+    send, block, mate_plane, cross_plane = call(
+        open_kernel,
+        [(count, tall, LANES), (9 * chunk, ny * nz), plane, plane],
+        [sums, (3 * chunk * ny, LANES)],
+        "open_windows",
+        4,
+        1 << 22,
+        *fields,
+        zone_labels,
+        zone_resistivity_inverse,
+        *flat,
+    )
+    block_mate = lax.ppermute(block, "slab", mates)
+    block_cross = lax.ppermute(block, "slab", across)
+    halo_mate = lax.ppermute(mate_plane, "slab", mates)
+    halo_cross = lax.ppermute(cross_plane, "slab", across)
+    packed = (nz, ny // 2, 8 * chunk)
+    shapes = [a.shape for a in fields]
+    for step_index in range(STEPS):
+        first, last = step_index == 0, step_index == STEPS - 1
+        arrived = lax.all_to_all(send, "slab", 0, 0, tiled=True)
+        kept = () if first else (potential,)
+        potential, loads = call(
+            functools.partial(solve_kernel, chunk, ny, nz, first),
+            [(3 * narrow, ny * nz) if first else (3 * chunk * ny, nz), packed],
+            [(2 if first else 1, ny * nz, LANES), (nz * ny // 2, LANES)]
+            + ([] if first else [(3 * chunk * ny, LANES)]),
+            "sweeps",
+            None,
+            1 << 22,
+            arrived,
+            block,
+            block_mate,
+            block_cross,
+            *kept,
+        )
+        loads = lax.all_to_all(loads, "slab", 0, 0, tiled=True)
+        scratch = [(6, 2, rows + 16, wide), sums]
+        if last:
+            fields = call(
+                functools.partial(flow_kernel, True),
+                shapes,
+                scratch,
+                "flow_last",
+                None,
+                1 << 22,
+                *fields,
+                halo_mate,
+                halo_cross,
+                loads,
+            )
+        else:
+            *fields, send, mate_plane, cross_plane = call(
+                functools.partial(flow_kernel, False),
+                shapes + [(count, ny, LANES), plane, plane],
+                scratch + [sums],
+                "flow_first",
+                7,
+                1 << 22,
+                *fields,
+                halo_mate,
+                halo_cross,
+                loads,
+                zone_labels,
+                zone_resistivity_inverse,
+            )
+            halo_mate = lax.ppermute(mate_plane, "slab", mates)
+            halo_cross = lax.ppermute(cross_plane, "slab", across)
+    return (*fields, potential.reshape(imposed_induction.shape))
+
+
+def on_device(*arrays):
+    count = lax.axis_size("slab")
+    _, chunk, ny, nz = arrays[5].shape
+    planes, rows, wide = arrays[1].shape
+    narrow = chunk + 2 * (HALO - SWEEPS)
+    fits = (
+        STEPS == 2
+        and planes == 2
+        and nz == count
+        and count % 2 == 0
+        and chunk >= HALO
+        and chunk % 8 == 0
+        and ny % 16 == 0
+        and 4 * narrow == LANES
+        and 8 * chunk == LANES
+        and nz * ny == 2 * LANES
+        and wide % (2 * LANES) == 0
+    )
+    return window_plan(*arrays) if fits else per_sweep_plan(*arrays)
+
+
 def solution(mesh):
     return jax.shard_map(
         on_device,

time: 318 us -> 84.6 us (0.27)
  starting transfers between devices: 146 us -> 28.3 us
  local copies, waits for them, and re-layouts: 102 us -> 2.2 us
  other arithmetic: 52.2 us -> 0 us
  blocking collectives: 0 us -> 23.9 us
  Pallas kernels: 0 us -> 19.3 us
  waiting for transfers between devices: 13.8 us -> 9.6 us
    ppermute x36 -> x6, starting transfers between devices: 115 us -> 6.88 us  [the longest x1 4.44 us: window_plan(): block_mate = lax.ppermute(block, 'slab', mates)]
    broadcast_in_dim x12 -> x0, local copies, waits for them, and re-layouts: 46.2 us -> none  [prolong(): jnp.broadcast_to(block[:, :, None, :, None, :, None], (comps, depth, 2, r...]
    reduce_sum x4 -> x0, local copies, waits for them, and re-layouts: 39 us -> none  [reduce_onto_parent(): return jnp.mean(shaped, axis=(2, 4, 6))]
    all_to_all x0 -> x2, blocking collectives: none -> 23.9 us  [the longest x1 12.7 us: window_plan(): arrived = lax.all_to_all(send, 'slab', 0, 0, tiled=True)]
    reduce_sum x12 -> x0, other arithmetic: 20.3 us -> none  [the longest x7 18.3 us: reduce_onto_parent(): return jnp.mean(shaped, axis=(2, 4, 6))]
    pallas_call x0 -> x5, Pallas kernels: none -> 19.3 us  [call(): pl.pallas_call(kernel, out_shape=[jax.ShapeDtypeStruct(s, jnp.float32) fo...]
    all_to_all x4 -> x2, starting transfers between devices: 30.3 us -> 21.5 us  [the longest x1 13.9 us: window_plan(): loads = lax.all_to_all(loads, 'slab', 0, 0, tiled=True)]
    unnamed x98 -> x18, local copies, waits for them, and re-layouts: 10.5 us -> 2.2 us
  transfers between devices with their start and end apart: 40 -> 8, of which waited for: 12 -> 3; matrix products, arithmetic and copies ran while one was open for 35% -> 0% of each run, Pallas kernels for 0% -> 9%
where the time goes in v1:
time: 84.6 us; the launch traced here: 84 us
  starting transfers between devices  28.3 us (33%)
  blocking collectives  23.9 us (28%)
  Pallas kernels  19.3 us (23%)
  waiting for transfers between devices  9.6 us (11%)
  local copies, waits for them, and re-layouts  2.2 us (3%)
    pallas_call x5, Pallas kernels, call(): pl.pallas_call(kernel, out_shape=[jax.ShapeDtypeStruct(s, jnp.float32) fo...  19.3 us
    all_to_all x1, starting transfers between devices, window_plan(): loads = lax.all_to_all(loads, 'slab', 0, 0, tiled=True)  13.9 us
    all_to_all x1, blocking collectives, window_plan(): arrived = lax.all_to_all(send, 'slab', 0, 0, tiled=True)  12.7 us
    all_to_all x1, blocking collectives, window_plan(): loads = lax.all_to_all(loads, 'slab', 0, 0, tiled=True)  11.1 us
    all_to_all x1, starting transfers between devices, window_plan(): arrived = lax.all_to_all(send, 'slab', 0, 0, tiled=True)  7.55 us
    all_to_all x1, waiting for transfers between devices, window_plan(): loads = lax.all_to_all(loads, 'slab', 0, 0, tiled=True)  6.85 us
    ppermute x1, starting transfers between devices, window_plan(): block_mate = lax.ppermute(block, 'slab', mates)  4.44 us
    unnamed x18, local copies, waits for them, and re-layouts  2.2 us
  transfers between devices with their start and end apart: 8, of which 3 were waited for; matrix products, arithmetic and copies ran while one was open for 0% of the time, Pallas kernels for 9%

profile of v1, /device:TPU:0, one launch (start us, length us, event | category | flops | bytes accessed | tf_op | source)
XLA Modules:
  0.0 84.0 jit_solution(17580251226377391201)
XLA Ops:
  0.6 3.9 %open_windows.1 = (f32[16,24,128]{2,1,0:T(8,128)}, f32[144,256]{1,0:T(8,128)}, f32[6,32,512]{2,1,0:T(8,128)}, f32[6,32,512]{2,1,0:T(8,128)}) custom-call(f32[3,2,32,512]{3,2,1,0:T(8,128)} %refs_0_.1, f32[2,32,512]{2,1,0:T(8,128)} %refs_1_.1, f32[2,2,32,512]{3,2,1,0:T(8,128)} %refs_2_.1, s32[1,16,256]{2,1,0:T(8,128)} %refs_6_.1, f32[8]{0:T(128)} %refs_7_.1, ...), custom_call_target="tpu_custom_call" | custom-call | flops 4194304 | bytes 262144 | tf_op jit(solution)/shard_map/open_windows/pallas_call | solution.py:506
  4.5 7.6 %all-to-all-start = ((f32[16,24,128]{2,1,0:T(8,128)}), f32[16,24,128]{2,1,0:T(8,128)S(1)}, u32[]{:S(2)}, u32[]{:S(2)}) async-start(f32[16,24,128]{2,1,0:T(8,128)} %get-tuple-element.23), calls=%async_computation | async-start | bytes 393216 | tf_op jit(solution)/shard_map/all_to_all | solution.py:568
  12.1 0.4 collective-permute-start
  12.5 0.7 collective-permute-start.1
  13.2 0.7 collective-permute-start.3
  13.8 4.4 %collective-permute-start.2 = (f32[144,256]{1,0:T(8,128)S(1)}, f32[144,256]{1,0:T(8,128)S(1)}, u32[]{:S(2)}, u32[]{:S(2)}) collective-permute-start(f32[144,256]{1,0:T(8,128)S(1)} %copy-done.1), channel_id=1, source_target_pairs={{0,1},{1,0},{2,3},{3,2},{4,5},{5,4},{6,7},{7,6},{8,9},{9,8},{10,11... | collective-permute-start | bytes 442376 | tf_op jit(solution)/shard_map/ppermute | solution.py:560
  18.3 0.0 collective-permute-done.3.refs_3_
  18.3 1.0 %collective-permute-done.2.refs_2_ = f32[144,256]{1,0:T(8,128)S(1)} collective-permute-done((f32[144,256]{1,0:T(8,128)S(1)}, f32[144,256]{1,0:T(8,128)S(1)}, u32[]{:S(2)}, u32[]{:S(2)}) %collective-permute-start.2) | collective-permute-done | bytes 147488 | tf_op jit(solution)/shard_map/ppermute | solution.py:560
  19.3 1.7 %all-to-all-done.refs_0_ = f32[16,24,128]{2,1,0:T(8,128)S(1)} async-done(((f32[16,24,128]{2,1,0:T(8,128)}), f32[16,24,128]{2,1,0:T(8,128)S(1)}, u32[]{:S(2)}, u32[]{:S(2)}) %all-to-all-start) | async-done | bytes 196640 | tf_op jit(solution)/shard_map/all_to_all | solution.py:568
  21.0 0.7 copy-done
  21.7 3.8 %sweeps.2 = (f32[96,256]{1,0:T(8,128)}, f32[16,8,128]{2,1,0:T(8,128)}) custom-call(f32[16,24,128]{2,1,0:T(8,128)} %copy-done, f32[144,256]{1,0:T(8,128)} %get-tuple-element.24.refs_1_, f32[144,256]{1,0:T(8,128)} %copy-done.3, f32[144,256]{1,0:T(8,128)} %copy-done.2), custom_call_target="tpu_custom_call" | custom-call | flops 4194304 | bytes 262144 | tf_op jit(solution)/shard_map/sweeps/pallas_call | solution.py:506
  25.5 13.9 %all-to-all-start.1 = ((f32[16,8,128]{2,1,0:T(8,128)}), f32[16,8,128]{2,1,0:T(8,128)S(1)}, u32[]{:S(2)}, u32[]{:S(2)}) async-start(f32[16,8,128]{2,1,0:T(8,128)} %get-tuple-element.25), calls=%async_computation.1 | async-start | bytes 131072 | tf_op jit(solution)/shard_map/all_to_all | solution.py:584
  39.4 0.0 copy-start.4
  39.4 0.0 copy-start.5
  39.4 6.9 %all-to-all-done.1.refs_5_ = f32[16,8,128]{2,1,0:T(8,128)S(1)} async-done(((f32[16,8,128]{2,1,0:T(8,128)}), f32[16,8,128]{2,1,0:T(8,128)S(1)}, u32[]{:S(2)}, u32[]{:S(2)}) %all-to-all-start.1) | async-done | bytes 65568 | tf_op jit(solution)/shard_map/all_to_all | solution.py:584
  46.3 0.6 copy-done.8
  46.9 4.5 %flow_first.1 = (f32[3,2,32,512]{3,2,1,0:T(8,128)}, f32[2,32,512]{2,1,0:T(8,128)}, f32[2,2,32,512]{3,2,1,0:T(8,128)}, f32[16,16,128]{2,1,0:T(8,128)}, f32[6,32,512]{2,1,0:T(8,128)}, /*index=5*/f32[6,32,512]{2,1,0:T(8,128)}) custom-call(f32[3,2,32,512]{3,2,1,0:T(8,128)} %refs_0_.1, f32[2,32,512]{2,1,0:T(8,128)} %refs_1_.1, f32[2,2,32,512]{3,2,1,0:T(8,128)} %refs_2_.1, ...), custom_call_target="tpu_custom_call" | custom-call | flops 4194304 | bytes 262144 | tf_op jit(solution)/shard_map/flow_first/pallas_call | solution.py:506
  51.5 0.7 collective-permute-start.5
  52.2 12.7 %all_to_all.20.refs_0_ = f32[16,16,128]{2,1,0:T(8,128)} all-to-all(f32[16,16,128]{2,1,0:T(8,128)} %get-tuple-element.31), channel_id=1, replica_groups=mesh['groups'=2,'slab'=16] {'slab'}, dimensions={0} | all-to-all | bytes 262144 | tf_op jit(solution)/shard_map/all_to_all | solution.py:568
  64.9 3.5 %sweeps.3 = (f32[768,16]{1,0:T(8,128)}, f32[16,8,128]{2,1,0:T(8,128)}) custom-call(f32[16,16,128]{2,1,0:T(8,128)} %all_to_all.20.refs_0_, f32[144,256]{1,0:T(8,128)} %get-tuple-element.24.refs_1_, f32[144,256]{1,0:T(8,128)} %copy-done.3, f32[144,256]{1,0:T(8,128)} %copy-done.2, f32[96,256]{1,0:T(8,128)} %get-tuple-element.32.refs_4_), custom_call_target="tpu_custom_call" | custom-call | flops 4194304 | bytes 262144 | tf_op jit(solution)/shard_map/sweeps/pallas_call | solution.py:506
  68.4 11.1 %all_to_all.21.refs_5_ = f32[16,8,128]{2,1,0:T(8,128)} all-to-all(f32[16,8,128]{2,1,0:T(8,128)} %get-tuple-element.33), channel_id=1, replica_groups=mesh['groups'=2,'slab'=16] {'slab'}, dimensions={0} | all-to-all | bytes 131072 | tf_op jit(solution)/shard_map/all_to_all | solution.py:584
  79.6 0.8 copy-done.6
  80.3 0.1 copy-done.7
  80.4 3.6 %flow_last.1 = (f32[3,2,32,512]{3,2,1,0:T(8,128)}, f32[2,32,512]{2,1,0:T(8,128)}, f32[2,2,32,512]{3,2,1,0:T(8,128)}) custom-call(f32[3,2,32,512]{3,2,1,0:T(8,128)} %get-tuple-element.26.refs_0_, f32[2,32,512]{2,1,0:T(8,128)} %get-tuple-element.27.refs_1_, f32[2,2,32,512]{3,2,1,0:T(8,128)} %get-tuple-element.28.refs_2_, f32[6,32,512]{2,1,0:T(8,128)} %copy-done.6, ...), custom_call_target="tpu_custom_call" | custom-call | flops 4194304 | bytes 262144 | tf_op jit(solution)/shard_map/flow_last/pallas_call | solution.py:506
  (17 shorter events, 0.0 us)
Async XLA Ops:
  4.5 8.7 %copy-start.1 = (f32[144,256]{1,0:T(8,128)S(1)}, f32[144,256]{1,0:T(8,128)}, u32[]{:S(2)}) copy-start(f32[144,256]{1,0:T(8,128)} %get-tuple-element.24.refs_1_) | copy-start | bytes 442372
  4.5 16.5 %all-to-all-start = ((f32[16,24,128]{2,1,0:T(8,128)}), f32[16,24,128]{2,1,0:T(8,128)S(1)}, u32[]{:S(2)}, u32[]{:S(2)}) async-start(f32[16,24,128]{2,1,0:T(8,128)} %get-tuple-element.23), calls=%async_computation | async-start | bytes 393216 | tf_op jit(solution)/shard_map/all_to_all | solution.py:568
  12.1 27.3 %collective-permute-start = (f32[6,32,512]{2,1,0:T(8,128)}, f32[6,32,512]{2,1,0:T(8,128)S(1)}, u32[]{:S(2)}, u32[]{:S(2)}) collective-permute-start(f32[6,32,512]{2,1,0:T(8,128)} %get-tuple-element.21), channel_id=1, source_target_pairs={{0,1},{1,0},{2,3},{3,2},{4,5},{5,4},{6,7},{7,6},{8,9},{9,8},{10,11... | collective-permute-start | bytes 1179656 | tf_op jit(solution)/shard_map/ppermute | solution.py:562
  12.5 27.0 %collective-permute-start.1 = (f32[6,32,512]{2,1,0:T(8,128)}, f32[6,32,512]{2,1,0:T(8,128)S(1)}, u32[]{:S(2)}, u32[]{:S(2)}) collective-permute-start(f32[6,32,512]{2,1,0:T(8,128)} %get-tuple-element.22), channel_id=1, source_target_pairs={{1,2},{3,4},{5,6},{7,8},{9,10},{11,12},{13,14},{2,1},{4,3},{6,5},{... | collective-permute-start | bytes 1179656 | tf_op jit(solution)/shard_map/ppermute | solution.py:563
  13.2 5.1 %collective-permute-start.3 = (f32[144,256]{1,0:T(8,128)S(1)}, f32[144,256]{1,0:T(8,128)S(1)}, u32[]{:S(2)}, u32[]{:S(2)}) collective-permute-start(f32[144,256]{1,0:T(8,128)S(1)} %copy-done.1), channel_id=1, source_target_pairs={{1,2},{3,4},{5,6},{7,8},{9,10},{11,12},{13,14},{2,1},{4,3},{6,5},{... | collective-permute-start | bytes 442376 | tf_op jit(solution)/shard_map/ppermute | solution.py:561
  13.8 5.4 %collective-permute-start.2 = (f32[144,256]{1,0:T(8,128)S(1)}, f32[144,256]{1,0:T(8,128)S(1)}, u32[]{:S(2)}, u32[]{:S(2)}) collective-permute-start(f32[144,256]{1,0:T(8,128)S(1)} %copy-done.1), channel_id=1, source_target_pairs={{0,1},{1,0},{2,3},{3,2},{4,5},{5,4},{6,7},{7,6},{8,9},{9,8},{10,11... | collective-permute-start | bytes 442376 | tf_op jit(solution)/shard_map/ppermute | solution.py:560
  18.3 2.7 %copy-start.2 = (f32[144,256]{1,0:T(8,128)}, f32[144,256]{1,0:T(8,128)S(1)}, u32[]{:S(2)}) copy-start(f32[144,256]{1,0:T(8,128)S(1)} %collective-permute-done.3.refs_3_) | copy-start | bytes 442372
  19.3 1.7 %copy-start.3 = (f32[144,256]{1,0:T(8,128)}, f32[144,256]{1,0:T(8,128)S(1)}, u32[]{:S(2)}) copy-start(f32[144,256]{1,0:T(8,128)S(1)} %collective-permute-done.2.refs_2_) | copy-start | bytes 442372
  21.0 0.7 copy-start
  25.5 20.8 %all-to-all-start.1 = ((f32[16,8,128]{2,1,0:T(8,128)}), f32[16,8,128]{2,1,0:T(8,128)S(1)}, u32[]{:S(2)}, u32[]{:S(2)}) async-start(f32[16,8,128]{2,1,0:T(8,128)} %get-tuple-element.25), calls=%async_computation.1 | async-start | bytes 131072 | tf_op jit(solution)/shard_map/all_to_all | solution.py:584
  39.4 6.9 %copy-start.4 = (f32[6,32,512]{2,1,0:T(8,128)}, f32[6,32,512]{2,1,0:T(8,128)S(1)}, u32[]{:S(2)}) copy-start(f32[6,32,512]{2,1,0:T(8,128)S(1)} %collective-permute-done.refs_3_) | copy-start | bytes 1179652
  39.4 6.9 %copy-start.5 = (f32[6,32,512]{2,1,0:T(8,128)}, f32[6,32,512]{2,1,0:T(8,128)S(1)}, u32[]{:S(2)}) copy-start(f32[6,32,512]{2,1,0:T(8,128)S(1)} %collective-permute-done.1.refs_4_) | copy-start | bytes 1179652
  46.3 0.6 copy-start.8
  51.5 28.1 %collective-permute-start.4 = (f32[6,32,512]{2,1,0:T(8,128)}, f32[6,32,512]{2,1,0:T(8,128)S(1)}, u32[]{:S(2)}, u32[]{:S(2)}) collective-permute-start(f32[6,32,512]{2,1,0:T(8,128)} %get-tuple-element.29), channel_id=1, source_target_pairs={{0,1},{1,0},{2,3},{3,2},{4,5},{5,4},{6,7},{7,6},{8,9},{9,8},{10,11... | collective-permute-start | bytes 1179656 | tf_op jit(solution)/shard_map/ppermute | solution.py:614
  51.5 28.1 %collective-permute-start.5 = (f32[6,32,512]{2,1,0:T(8,128)}, f32[6,32,512]{2,1,0:T(8,128)S(1)}, u32[]{:S(2)}, u32[]{:S(2)}) collective-permute-start(f32[6,32,512]{2,1,0:T(8,128)} %get-tuple-element.30), channel_id=1, source_target_pairs={{1,2},{3,4},{5,6},{7,8},{9,10},{11,12},{13,14},{2,1},{4,3},{6,5},{... | collective-permute-start | bytes 1179656 | tf_op jit(solution)/shard_map/ppermute | solution.py:615
  79.5 0.8 copy-start.6
  79.5 0.9 %copy-start.7 = (f32[6,32,512]{2,1,0:T(8,128)}, f32[6,32,512]{2,1,0:T(8,128)S(1)}, u32[]{:S(2)}) copy-start(f32[6,32,512]{2,1,0:T(8,128)S(1)} %collective-permute-done.5.refs_4_) | copy-start | bytes 1179652

commit v2 on v1

--- a/solution.py
+++ b/solution.py
@@ -244,31 +244,47 @@
             )
 
 
-def open_kernel(
-    vel_ref,
-    heat_ref,
-    turb_ref,
-    labels_ref,
-    table_ref,
-    guess_ref,
-    applied_ref,
-    coil_ref,
-    send_ref,
-    block_ref,
-    mate_ref,
-    cross_ref,
-    sums_ref,
-    flat_ref,
-):
+def edge_kernel(vel_ref, heat_ref, turb_ref, guess_ref, applied_ref, coil_ref, mate_ref, cross_ref, flat_ref, sems):
     odd = lax.rem(lax.axis_index("slab"), 2)
-    planes = [(vel_ref, 0), (vel_ref, 1), (vel_ref, 2), (heat_ref, None), (turb_ref, 0), (turb_ref, 1)]
-    for f, (ref, comp) in enumerate(planes):
-        if comp is None:
-            mate_ref[f] = ref[1 - odd]
-            cross_ref[f] = ref[odd]
-        else:
-            mate_ref[f] = ref[comp, 1 - odd]
-            cross_ref[f] = ref[comp, odd]
+    rows = heat_ref.shape[1]
+    moves = []
+    for f in range(6):
+        for which, (out_ref, plane) in enumerate(((mate_ref, 1 - odd), (cross_ref, odd))):
+            if f < 3:
+                start = vel_ref.at[f, plane]
+            elif f == 3:
+                start = heat_ref.at[plane]
+            else:
+                start = turb_ref.at[f - 4, plane]
+            move = pltpu.make_async_copy(
+                start, out_ref.at[pl.ds(f * rows, rows)], sems.at[2 * f + which]
+            )
+            move.start()
+            moves.append(move)
+    pairs, nz = guess_ref.shape
+    chunk = (mate_ref.shape[0] - 6 * rows) // 5
+    ny = pairs // (3 * chunk)
+    lanes = ny * nz
+    for kind, ref in enumerate((guess_ref, applied_ref, coil_ref)):
+        flat_ref[:, kind * nz : (kind + 1) * nz] = ref[...]
+    lines = [flat_ref[pl.ds(y, 3 * chunk, stride=ny), :] for y in range(ny)]
+    for kind in range(3):
+        packed = jnp.concatenate([line[:, kind * nz : (kind + 1) * nz] for line in lines], 1)
+        for c in range(3):
+            row, lane = block_spot(3 * kind + c, rows, chunk, lanes)
+            piece = packed[c * chunk : (c + 1) * chunk]
+            mate_ref[row, lane] = piece
+            cross_ref[row, lane] = piece
+    for move in moves:
+        move.wait()
+
+
+def block_spot(index, rows, chunk, lanes):
+    row = 6 * rows + (index % 5) * chunk
+    return slice(row, row + chunk), slice(index // 5 * lanes, (index // 5 + 1) * lanes)
+
+
+def open_kernel(vel_ref, heat_ref, labels_ref, table_ref, send_ref, sums_ref):
     rows = heat_ref.shape[1]
     for t in range(sums_ref.shape[0]):
         at = slice(t * LANES, (t + 1) * LANES)
@@ -277,20 +293,10 @@
         sums_ref[t, 3 * rows :, :] = jnp.exp(
             -thermal_gradient_factor * heat_ref[0, :, at]
         ) + jnp.exp(-thermal_gradient_factor * heat_ref[1, :, at])
-    total, nz = guess_ref.shape
-    ny = labels_ref.shape[1]
-    stacked = total // ny
-    for kind, ref in enumerate((guess_ref, applied_ref, coil_ref)):
-        flat_ref[:, kind * nz : (kind + 1) * nz] = ref[...]
-    lines = [flat_ref[pl.ds(y, stacked, stride=ny), :] for y in range(ny)]
-    for kind in range(3):
-        block_ref[kind * stacked : (kind + 1) * stacked, :] = jnp.concatenate(
-            [line[:, kind * nz : (kind + 1) * nz] for line in lines], 1
-        )
     pack_windows(sums_ref, labels_ref, table_ref, send_ref, HALO)
 
 
-def solve_kernel(chunk, ny, nz, first, *refs):
+def solve_kernel(chunk, ny, nz, rows, first, *refs):
     if first:
         recv_ref, block_ref, mate_ref, cross_ref, pot_out, send_ref, wide_ref, turn_ref = refs
         halo = HALO
@@ -316,13 +322,13 @@
     def windowed(kind):
         found = []
         for c in range(3):
-            base = (kind * 3 + c) * chunk
-            mate, cross_side = mate_ref[base : base + chunk, :], cross_ref[base : base + chunk, :]
+            row, lane = block_spot(3 * kind + c, rows, chunk, ny * nz)
+            mate, cross_side = mate_ref[row, lane], cross_ref[row, lane]
             low = jnp.where(odd == 0, cross_side, mate)
             high = jnp.where(odd == 0, mate, cross_side)
             found.append(
                 jnp.concatenate(
-                    [low[chunk - halo :], block_ref[base : base + chunk, :], high[:halo]], 0
+                    [low[chunk - halo :], block_ref[row, lane], high[:halo]], 0
                 )
             )
         return found
@@ -429,7 +435,8 @@
             strain = jnp.zeros((8, wide), jnp.float32)
             for f in range(6):
                 here = center[f]
-                mate, cross_side = mate_ref[f, tile, :], cross_ref[f, tile, :]
+                spot = slice(f * rows + top, f * rows + top + 8)
+                mate, cross_side = mate_ref[spot, :], cross_ref[spot, :]
                 other = bordered_ref[f, 1 - plane, 8 + top : 16 + top, :]
                 if plane == 0:
                     z_minus, z_plus = jnp.where(odd == 0, cross_side, mate), other
@@ -492,25 +499,26 @@
     outs = [(vel_out, 0), (vel_out, 1), (vel_out, 2), (heat_out, None), (turb_out, 0), (turb_out, 1)]
     for f, (ref, comp) in enumerate(outs):
         if comp is None:
-            mate_out[f] = ref[1 - odd]
-            cross_out[f] = ref[odd]
+            mate_out[f * rows : (f + 1) * rows, :] = ref[1 - odd]
+            cross_out[f * rows : (f + 1) * rows, :] = ref[odd]
         else:
-            mate_out[f] = ref[comp, 1 - odd]
-            cross_out[f] = ref[comp, odd]
+            mate_out[f * rows : (f + 1) * rows, :] = ref[comp, 1 - odd]
+            cross_out[f * rows : (f + 1) * rows, :] = ref[comp, odd]
     pack_windows(sums_ref, labels_ref, table_ref, send_ref, HALO - SWEEPS)
 
 
-def call(kernel, outs, scratch, name, table_at, cost, *operands):
+def call(kernel, outs, scratch, name, spaces, grant, cost, *operands):
     vmem = pl.BlockSpec(memory_space=pltpu.VMEM)
-    smem = pl.BlockSpec(memory_space=pltpu.SMEM)
+    special = {"s": pl.BlockSpec(memory_space=pltpu.SMEM), "a": pl.BlockSpec(memory_space=pl.ANY)}
     return pl.pallas_call(
         kernel,
         out_shape=[jax.ShapeDtypeStruct(s, jnp.float32) for s in outs],
-        in_specs=[smem if i == table_at else vmem for i in range(len(operands))],
+        in_specs=[special.get(spaces.get(i), vmem) for i in range(len(operands))],
         out_specs=[vmem] * len(outs),
-        scratch_shapes=[pltpu.VMEM(s, jnp.float32) for s in scratch],
+        scratch_shapes=[pltpu.VMEM(s, jnp.float32) if isinstance(s, tuple) else s for s in scratch],
         name=name,
-        cost_estimate=pl.CostEstimate(flops=cost, bytes_accessed=4 * cost // 64, transcendentals=0),
+        cost_estimate=pl.CostEstimate(flops=cost, bytes_accessed=cost, transcendentals=0),
+        compiler_params=pltpu.CompilerParams(vmem_limit_bytes=grant << 20),
     )(*operands)
 
 
@@ -542,25 +550,38 @@
     ]
     window, narrow = chunk + 2 * HALO, chunk + 2 * (HALO - SWEEPS)
     tall = ny + ny // 2 if 4 * window > LANES else ny
-    plane = (6, rows, wide)
+    edge = (6 * rows, wide)
+    joint = (6 * rows + 5 * chunk, wide)
     sums = (wide // LANES, 4 * rows, LANES)
     fields = (melt_speeds, heat_state, eddy_quantities)
-    send, block, mate_plane, cross_plane = call(
+    mate, cross_side = call(
+        edge_kernel,
+        [joint, joint],
+        [(3 * chunk * ny, LANES), pltpu.SemaphoreType.DMA((12,))],
+        "edges",
+        {0: "a", 1: "a", 2: "a"},
+        8,
+        1 << 20,
+        *fields,
+        *flat,
+    )
+    block = mate
+    mate = lax.ppermute(mate, "slab", mates)
+    cross_side = lax.ppermute(cross_side, "slab", across)
+    block_mate, block_cross = mate, cross_side
+    (send,) = call(
         open_kernel,
-        [(count, tall, LANES), (9 * chunk, ny * nz), plane, plane],
-        [sums, (3 * chunk * ny, LANES)],
+        [(count, tall, LANES)],
+        [sums],
         "open_windows",
-        4,
+        {3: "s"},
+        8,
         1 << 22,
-        *fields,
+        melt_speeds,
+        heat_state,
         zone_labels,
         zone_resistivity_inverse,
-        *flat,
-    )
-    block_mate = lax.ppermute(block, "slab", mates)
-    block_cross = lax.ppermute(block, "slab", across)
-    halo_mate = lax.ppermute(mate_plane, "slab", mates)
-    halo_cross = lax.ppermute(cross_plane, "slab", across)
+    )
     packed = (nz, ny // 2, 8 * chunk)
     shapes = [a.shape for a in fields]
     for step_index in range(STEPS):
@@ -568,12 +589,13 @@
         arrived = lax.all_to_all(send, "slab", 0, 0, tiled=True)
         kept = () if first else (potential,)
         potential, loads = call(
-            functools.partial(solve_kernel, chunk, ny, nz, first),
+            functools.partial(solve_kernel, chunk, ny, nz, rows, first),
             [(3 * narrow, ny * nz) if first else (3 * chunk * ny, nz), packed],
             [(2 if first else 1, ny * nz, LANES), (nz * ny // 2, LANES)]
             + ([] if first else [(3 * chunk * ny, LANES)]),
             "sweeps",
-            None,
+            {},
+            8,
             1 << 22,
             arrived,
             block,
@@ -589,30 +611,32 @@
                 shapes,
                 scratch,
                 "flow_last",
-                None,
+                {},
+                12,
                 1 << 22,
                 *fields,
-                halo_mate,
-                halo_cross,
+                mate,
+                cross_side,
                 loads,
             )
         else:
-            *fields, send, mate_plane, cross_plane = call(
+            *fields, send, mate, cross_side = call(
                 functools.partial(flow_kernel, False),
-                shapes + [(count, ny, LANES), plane, plane],
+                shapes + [(count, ny, LANES), edge, edge],
                 scratch + [sums],
                 "flow_first",
-                7,
+                {7: "s"},
+                12,
                 1 << 22,
                 *fields,
-                halo_mate,
-                halo_cross,
+                mate,
+                cross_side,
                 loads,
                 zone_labels,
                 zone_resistivity_inverse,
             )
-            halo_mate = lax.ppermute(mate_plane, "slab", mates)
-            halo_cross = lax.ppermute(cross_plane, "slab", across)
+            mate = lax.ppermute(mate, "slab", mates)
+            cross_side = lax.ppermute(cross_side, "slab", across)
     return (*fields, potential.reshape(imposed_induction.shape))
 
 
@@ -632,7 +656,7 @@
         and 4 * narrow == LANES
         and 8 * chunk == LANES
         and nz * ny == 2 * LANES
-        and wide % (2 * LANES) == 0
+        and wide == 2 * ny * nz
     )
     return window_plan(*arrays) if fits else per_sweep_plan(*arrays)
 

time: 84.6 us -> 74.1 us (0.88)
  blocking collectives: 23.9 us -> 49.2 us
  starting transfers between devices: 28.3 us -> 5.84 us
  waiting for transfers between devices: 9.6 us -> 0.01 us
  Pallas kernels: 19.3 us -> 12 us
  local copies, waits for them, and re-layouts: 2.2 us -> 5.86 us
    all_to_all x2 -> x0, starting transfers between devices: 21.5 us -> none  [the longest x1 13.9 us: window_plan(): loads = lax.all_to_all(loads, 'slab', 0, 0, tiled=True)]
    all_to_all x1 -> x2, blocking collectives: 12.7 us -> 26.2 us  [window_plan(): arrived = lax.all_to_all(send, 'slab', 0, 0, tiled=True)]
    all_to_all x1 -> x2, blocking collectives: 11.1 us -> 23 us  [window_plan(): loads = lax.all_to_all(loads, 'slab', 0, 0, tiled=True)]
    all_to_all x2 -> x0, waiting for transfers between devices: 8.59 us -> none  [the longest x1 6.85 us: window_plan(): loads = lax.all_to_all(loads, 'slab', 0, 0, tiled=True)]
    pallas_call x5 -> x6, Pallas kernels: 19.3 us -> 12 us  [call(): pl.pallas_call(kernel, out_shape=[jax.ShapeDtypeStruct(s, jnp.float32) fo...]
    unnamed x18 -> x22, local copies, waits for them, and re-layouts: 2.2 us -> 5.86 us
    ppermute x6 -> x4, starting transfers between devices: 6.88 us -> 5.84 us  [the longest x2 4.46 us: window_plan(): mate = lax.ppermute(mate, 'slab', mates)]
    ppermute x6 -> x4, waiting for transfers between devices: 1.02 us -> 0.01 us  [the longest x2 0.01 us: window_plan(): cross_side = lax.ppermute(cross_side, 'slab', across)]
  transfers between devices with their start and end apart: 8 -> 4, of which waited for: 3 -> 0; matrix products, arithmetic and copies ran while one was open for 0% -> 0% of each run, Pallas kernels for 9% -> 5%
where the time goes in v2:
time: 74.1 us; the launch traced here: 73.6 us
  blocking collectives  49.2 us (66%)
  Pallas kernels  12 us (16%)
  local copies, waits for them, and re-layouts  5.86 us (8%)
  starting transfers between devices  5.84 us (8%)
    all_to_all x2, blocking collectives, window_plan(): arrived = lax.all_to_all(send, 'slab', 0, 0, tiled=True)  26.2 us
    all_to_all x2, blocking collectives, window_plan(): loads = lax.all_to_all(loads, 'slab', 0, 0, tiled=True)  23 us
    pallas_call x6, Pallas kernels, call(): pl.pallas_call(kernel, out_shape=[jax.ShapeDtypeStruct(s, jnp.float32) fo...  12 us
    unnamed x22, local copies, waits for them, and re-layouts  5.86 us
    ppermute x2, starting transfers between devices, window_plan(): mate = lax.ppermute(mate, 'slab', mates)  4.46 us
  transfers between devices with their start and end apart: 4, of which 0 were waited for; matrix products, arithmetic and copies ran while one was open for 0% of the time, Pallas kernels for 5%

profile of v2, /device:TPU:0, one launch (start us, length us, event | category | flops | bytes accessed | tf_op | source)
XLA Modules:
  0.0 73.6 jit_solution(3731412618547710875)
XLA Ops:
  0.6 0.0 copy-start
  0.6 1.0 %copy-done = f32[3,2,32,512]{3,2,1,0:T(8,128)S(1)} copy-done((f32[3,2,32,512]{3,2,1,0:T(8,128)S(1)}, f32[3,2,32,512]{3,2,1,0:T(8,128)}, u32[]{:S(2)}) %copy-start) | copy-done | bytes 393240
  1.6 0.9 %copy-done.2 = f32[2,32,512]{2,1,0:T(8,128)S(1)} copy-done((f32[2,32,512]{2,1,0:T(8,128)S(1)}, f32[2,32,512]{2,1,0:T(8,128)}, u32[]{:S(2)}) %copy-start.2) | copy-done | bytes 131096
  2.5 0.9 %copy-done.4 = f32[2,2,32,512]{3,2,1,0:T(8,128)S(1)} copy-done((f32[2,2,32,512]{3,2,1,0:T(8,128)S(1)}, f32[2,2,32,512]{3,2,1,0:T(8,128)}, u32[]{:S(2)}) %copy-start.4) | copy-done | bytes 262168
  3.5 1.0 %copy-done.6 = f32[3,16,16,16]{3,2,1,0:T(8,128)S(1)} copy-done((f32[3,16,16,16]{3,2,1,0:T(8,128)S(1)}, f32[3,16,16,16]{3,2,1,0:T(8,128)}, u32[]{:S(2)}) %copy-start.6) | copy-done | bytes 49176
  4.5 1.0 %copy-done.7 = f32[3,16,16,16]{3,2,1,0:T(8,128)S(1)} copy-done((f32[3,16,16,16]{3,2,1,0:T(8,128)S(1)}, f32[3,16,16,16]{3,2,1,0:T(8,128)}, u32[]{:S(2)}) %copy-start.7) | copy-done | bytes 49176
  5.5 1.0 %copy-done.8 = f32[3,16,16,16]{3,2,1,0:T(8,128)S(1)} copy-done((f32[3,16,16,16]{3,2,1,0:T(8,128)S(1)}, f32[3,16,16,16]{3,2,1,0:T(8,128)}, u32[]{:S(2)}) %copy-start.8) | copy-done | bytes 49176
  6.5 1.8 %edges.1 = (f32[272,512]{1,0:T(8,128)S(1)}, f32[272,512]{1,0:T(8,128)S(1)}) custom-call(f32[3,2,32,512]{3,2,1,0:T(8,128)S(1)} %copy-done, f32[2,32,512]{2,1,0:T(8,128)S(1)} %copy-done.2, f32[2,2,32,512]{3,2,1,0:T(8,128)S(1)} %copy-done.4, f32[768,16]{1,0:T(8,128)S(1)} %bitcast.4, f32[768,16]{1,0:T(8,128)S(1)} %bitcast.5, f32[768,16]{1,0:T(8,128)S(1)} %bitcast.6), custom_call_target="tpu_custom_call" | custom-call | flops 1048576 | bytes 1048576 | tf_op jit(solution)/shard_map/edges/pallas_call | solution.py:513
  8.2 0.0 copy-start.10
  8.3 0.7 collective-permute-start.1
  9.0 4.4 %collective-permute-start = (f32[272,512]{1,0:T(8,128)S(1)}, f32[272,512]{1,0:T(8,128)S(1)}, u32[]{:S(2)}, u32[]{:S(2)}) collective-permute-start(f32[272,512]{1,0:T(8,128)S(1)} %get-tuple-element.19.refs_1_), channel_id=1, source_target_pairs={{0,1},{1,0},{2,3},{3,2},{4,5},{5,4},{6,7},{7,6},{8,9},{9,8},{10,11... | collective-permute-start | bytes 1671176 | tf_op jit(solution)/shard_map/ppermute | solution.py:569
  13.4 1.1 %open_windows.1 = f32[16,24,128]{2,1,0:T(8,128)S(1)} custom-call(f32[3,2,32,512]{3,2,1,0:T(8,128)S(1)} %copy-done, f32[2,32,512]{2,1,0:T(8,128)S(1)} %copy-done.2, s32[1,16,256]{2,1,0:T(8,128)S(1)} %copy-done.9, f32[8]{0:T(128)S(1)} %copy-done.10), custom_call_target="tpu_custom_call" | custom-call | flops 4194304 | bytes 4194304 | tf_op jit(solution)/shard_map/open_windows/pallas_call | solution.py:513
  14.4 13.7 %all_to_all.20.refs_0_ = f32[16,24,128]{2,1,0:T(8,128)S(1)} all-to-all(f32[16,24,128]{2,1,0:T(8,128)S(1)} %open_windows.1), channel_id=1, replica_groups=mesh['groups'=2,'slab'=16] {'slab'}, dimensions={0} | all-to-all | bytes 393216 | tf_op jit(solution)/shard_map/all_to_all | solution.py:589
  28.2 0.0 copy-start.5
  28.2 2.0 %sweeps.2 = (f32[96,256]{1,0:T(8,128)S(1)}, f32[16,8,128]{2,1,0:T(8,128)S(1)}) custom-call(f32[16,24,128]{2,1,0:T(8,128)S(1)} %all_to_all.20.refs_0_, f32[272,512]{1,0:T(8,128)S(1)} %get-tuple-element.19.refs_1_, f32[272,512]{1,0:T(8,128)S(1)} %collective-permute-done.refs_2_.refs_3_, f32[272,512]{1,0:T(8,128)S(1)} %collective-permute-done.1.refs_3_.refs_4_), custom_call_target="tpu_custom_call" | custom-call | flops 4194304 | bytes 4194304 | tf_op jit(solution)/shard_map/sweeps/pallas_call | solution.py:513
  30.2 0.0 copy-start.3
  30.2 12.2 %all_to_all.21.refs_5_ = f32[16,8,128]{2,1,0:T(8,128)S(1)} all-to-all(f32[16,8,128]{2,1,0:T(8,128)S(1)} %get-tuple-element.21), channel_id=1, replica_groups=mesh['groups'=2,'slab'=16] {'slab'}, dimensions={0} | all-to-all | bytes 131072 | tf_op jit(solution)/shard_map/all_to_all | solution.py:606
  42.5 2.6 %flow_first.1 = (f32[3,2,32,512]{3,2,1,0:T(8,128)S(1)}, f32[2,32,512]{2,1,0:T(8,128)S(1)}, f32[2,2,32,512]{3,2,1,0:T(8,128)S(1)}, f32[16,16,128]{2,1,0:T(8,128)S...) custom-call(f32[3,2,32,512]{3,2,1,0:T(8,128)S(1)} %copy-done.1, f32[2,32,512]{2,1,0:T(8,128)S(1)} %copy-done.3, ...), custom_call_target="tpu_custom_call" | custom-call | flops 4194304 | bytes 4194304 | tf_op jit(solution)/shard_map/flow_first/pallas_call | solution.py:513
  45.1 0.1 collective-permute-start.2
  45.1 0.7 collective-permute-start.3
  45.8 12.4 %all_to_all.22.refs_0_ = f32[16,16,128]{2,1,0:T(8,128)S(1)} all-to-all(f32[16,16,128]{2,1,0:T(8,128)S(1)} %get-tuple-element.27), channel_id=1, replica_groups=mesh['groups'=2,'slab'=16] {'slab'}, dimensions={0} | all-to-all | bytes 262144 | tf_op jit(solution)/shard_map/all_to_all | solution.py:589
  58.2 2.3 %sweeps.3 = (f32[768,16]{1,0:T(8,128)}, f32[16,8,128]{2,1,0:T(8,128)S(1)}) custom-call(f32[16,16,128]{2,1,0:T(8,128)S(1)} %all_to_all.22.refs_0_, f32[272,512]{1,0:T(8,128)S(1)} %get-tuple-element.19.refs_1_, f32[272,512]{1,0:T(8,128)S(1)} %collective-permute-done.refs_2_.refs_3_, f32[272,512]{1,0:T(8,128)S(1)} %collective-permute-done.1.refs_3_.refs_4_, ...), custom_call_target="tpu_custom_call" | custom-call | flops 4194304 | bytes 4194304 | tf_op jit(solution)/shard_map/sweeps/pallas_call | solution.py:513
  60.5 10.8 %all_to_all.23.refs_5_ = f32[16,8,128]{2,1,0:T(8,128)S(1)} all-to-all(f32[16,8,128]{2,1,0:T(8,128)S(1)} %get-tuple-element.29), channel_id=1, replica_groups=mesh['groups'=2,'slab'=16] {'slab'}, dimensions={0} | all-to-all | bytes 131072 | tf_op jit(solution)/shard_map/all_to_all | solution.py:606
  71.4 2.3 %flow_last.1 = (f32[3,2,32,512]{3,2,1,0:T(8,128)}, f32[2,32,512]{2,1,0:T(8,128)}, f32[2,2,32,512]{3,2,1,0:T(8,128)}) custom-call(f32[3,2,32,512]{3,2,1,0:T(8,128)S(1)} %get-tuple-element.22.refs_0_, f32[2,32,512]{2,1,0:T(8,128)S(1)} %get-tuple-element.23.refs_1_, f32[2,2,32,512]{3,2,1,0:T(8,128)S(1)} %get-tuple-element.24.refs_2_, ...), custom_call_target="tpu_custom_call" | custom-call | flops 4194304 | bytes 4194304 | tf_op jit(solution)/shard_map/flow_last/pallas_call | solution.py:513
  (16 shorter events, 0.0 us)
Async XLA Ops:
  0.6 1.0 %copy-start = (f32[3,2,32,512]{3,2,1,0:T(8,128)S(1)}, f32[3,2,32,512]{3,2,1,0:T(8,128)}, u32[]{:S(2)}) copy-start(f32[3,2,32,512]{3,2,1,0:T(8,128)} %refs_0_.1) | copy-start | bytes 1179652
  1.6 0.9 %copy-start.2 = (f32[2,32,512]{2,1,0:T(8,128)S(1)}, f32[2,32,512]{2,1,0:T(8,128)}, u32[]{:S(2)}) copy-start(f32[2,32,512]{2,1,0:T(8,128)} %refs_1_.1) | copy-start | bytes 393220
  2.5 0.9 %copy-start.4 = (f32[2,2,32,512]{3,2,1,0:T(8,128)S(1)}, f32[2,2,32,512]{3,2,1,0:T(8,128)}, u32[]{:S(2)}) copy-start(f32[2,2,32,512]{3,2,1,0:T(8,128)} %refs_2_.1) | copy-start | bytes 786436
  3.5 1.0 %copy-start.6 = (f32[3,16,16,16]{3,2,1,0:T(8,128)S(1)}, f32[3,16,16,16]{3,2,1,0:T(8,128)}, u32[]{:S(2)}) copy-start(f32[3,16,16,16]{3,2,1,0:T(8,128)} %param.15) | copy-start | bytes 147460
  4.5 1.0 %copy-start.7 = (f32[3,16,16,16]{3,2,1,0:T(8,128)S(1)}, f32[3,16,16,16]{3,2,1,0:T(8,128)}, u32[]{:S(2)}) copy-start(f32[3,16,16,16]{3,2,1,0:T(8,128)} %param.13) | copy-start | bytes 147460
  5.5 1.0 %copy-start.8 = (f32[3,16,16,16]{3,2,1,0:T(8,128)S(1)}, f32[3,16,16,16]{3,2,1,0:T(8,128)}, u32[]{:S(2)}) copy-start(f32[3,16,16,16]{3,2,1,0:T(8,128)} %param.14) | copy-start | bytes 147460
  6.5 6.9 %copy-start.9 = (s32[1,16,256]{2,1,0:T(8,128)S(1)}, s32[1,16,256]{2,1,0:T(8,128)}, u32[]{:S(2)}) copy-start(s32[1,16,256]{2,1,0:T(8,128)} %refs_6_.1) | copy-start | bytes 49156
  8.2 5.1 %copy-start.10 = (f32[8]{0:T(128)S(1)}, f32[8]{0:T(128)}, u32[]{:S(2)}) copy-start(f32[8]{0:T(128)} %refs_7_.1) | copy-start | bytes 100
  8.3 19.9 %collective-permute-start.1 = (f32[272,512]{1,0:T(8,128)S(1)}, f32[272,512]{1,0:T(8,128)S(1)}, u32[]{:S(2)}, u32[]{:S(2)}) collective-permute-start(f32[272,512]{1,0:T(8,128)S(1)} %get-tuple-element.20), channel_id=1, source_target_pairs={{1,2},{3,4},{5,6},{7,8},{9,10},{11,12},{13,14},{2,1},{4,3},{6,5},{... | collective-permute-start | bytes 1671176 | tf_op jit(solution)/shard_map/ppermute | solution.py:570
  9.0 19.2 %collective-permute-start = (f32[272,512]{1,0:T(8,128)S(1)}, f32[272,512]{1,0:T(8,128)S(1)}, u32[]{:S(2)}, u32[]{:S(2)}) collective-permute-start(f32[272,512]{1,0:T(8,128)S(1)} %get-tuple-element.19.refs_1_), channel_id=1, source_target_pairs={{0,1},{1,0},{2,3},{3,2},{4,5},{5,4},{6,7},{7,6},{8,9},{9,8},{10,11... | collective-permute-start | bytes 1671176 | tf_op jit(solution)/shard_map/ppermute | solution.py:569
  28.2 14.3 %copy-start.1 = (f32[3,2,32,512]{3,2,1,0:T(8,128)S(1)}, f32[3,2,32,512]{3,2,1,0:T(8,128)}, u32[]{:S(2)}) copy-start(f32[3,2,32,512]{3,2,1,0:T(8,128)} %refs_0_.1) | copy-start | bytes 1179652
  28.2 14.3 %copy-start.5 = (f32[2,2,32,512]{3,2,1,0:T(8,128)S(1)}, f32[2,2,32,512]{3,2,1,0:T(8,128)}, u32[]{:S(2)}) copy-start(f32[2,2,32,512]{3,2,1,0:T(8,128)} %refs_2_.1) | copy-start | bytes 786436
  30.2 12.3 %copy-start.3 = (f32[2,32,512]{2,1,0:T(8,128)S(1)}, f32[2,32,512]{2,1,0:T(8,128)}, u32[]{:S(2)}) copy-start(f32[2,32,512]{2,1,0:T(8,128)} %refs_1_.1) | copy-start | bytes 393220
  45.1 26.3 %collective-permute-start.2 = (f32[192,512]{1,0:T(8,128)S(1)}, f32[192,512]{1,0:T(8,128)S(1)}, u32[]{:S(2)}, u32[]{:S(2)}) collective-permute-start(f32[192,512]{1,0:T(8,128)S(1)} %get-tuple-element.25), channel_id=1, source_target_pairs={{0,1},{1,0},{2,3},{3,2},{4,5},{5,4},{6,7},{7,6},{8,9},{9,8},{10,11... | collective-permute-start | bytes 1179656 | tf_op jit(solution)/shard_map/ppermute | solution.py:638
  45.1 26.2 %collective-permute-start.3 = (f32[192,512]{1,0:T(8,128)S(1)}, f32[192,512]{1,0:T(8,128)S(1)}, u32[]{:S(2)}, u32[]{:S(2)}) collective-permute-start(f32[192,512]{1,0:T(8,128)S(1)} %get-tuple-element.26), channel_id=1, source_target_pairs={{1,2},{3,4},{5,6},{7,8},{9,10},{11,12},{13,14},{2,1},{4,3},{6,5},{... | collective-permute-start | bytes 1179656 | tf_op jit(solution)/shard_map/ppermute | solution.py:639

commit v3 on v2

--- a/solution.py
+++ b/solution.py
@@ -244,29 +244,37 @@
             )
 
 
-def edge_kernel(vel_ref, heat_ref, turb_ref, guess_ref, applied_ref, coil_ref, mate_ref, cross_ref, flat_ref, sems):
+def edge_kernel(
+    vel_ref,
+    heat_ref,
+    turb_ref,
+    guess_ref,
+    applied_ref,
+    coil_ref,
+    mate_ref,
+    cross_ref,
+    vel_out,
+    heat_out,
+    turb_out,
+    flat_ref,
+    raw_ref,
+    sems,
+):
     odd = lax.rem(lax.axis_index("slab"), 2)
     rows = heat_ref.shape[1]
-    moves = []
-    for f in range(6):
-        for which, (out_ref, plane) in enumerate(((mate_ref, 1 - odd), (cross_ref, odd))):
-            if f < 3:
-                start = vel_ref.at[f, plane]
-            elif f == 3:
-                start = heat_ref.at[plane]
-            else:
-                start = turb_ref.at[f - 4, plane]
-            move = pltpu.make_async_copy(
-                start, out_ref.at[pl.ds(f * rows, rows)], sems.at[2 * f + which]
-            )
-            move.start()
-            moves.append(move)
-    pairs, nz = guess_ref.shape
+    pairs = [(guess_ref, raw_ref.at[0]), (applied_ref, raw_ref.at[1]), (coil_ref, raw_ref.at[2])]
+    pairs += [(vel_ref, vel_out), (heat_ref, heat_out), (turb_ref, turb_out)]
+    moves = [pltpu.make_async_copy(a, b, sems.at[i]) for i, (a, b) in enumerate(pairs)]
+    for move in moves:
+        move.start()
+    for move in moves[:3]:
+        move.wait()
+    total, nz = guess_ref.shape
     chunk = (mate_ref.shape[0] - 6 * rows) // 5
-    ny = pairs // (3 * chunk)
+    ny = total // (3 * chunk)
     lanes = ny * nz
-    for kind, ref in enumerate((guess_ref, applied_ref, coil_ref)):
-        flat_ref[:, kind * nz : (kind + 1) * nz] = ref[...]
+    for kind in range(3):
+        flat_ref[:, kind * nz : (kind + 1) * nz] = raw_ref[kind]
     lines = [flat_ref[pl.ds(y, 3 * chunk, stride=ny), :] for y in range(ny)]
     for kind in range(3):
         packed = jnp.concatenate([line[:, kind * nz : (kind + 1) * nz] for line in lines], 1)
@@ -275,8 +283,22 @@
             piece = packed[c * chunk : (c + 1) * chunk]
             mate_ref[row, lane] = piece
             cross_ref[row, lane] = piece
-    for move in moves:
+    for move in moves[3:]:
         move.wait()
+    split_planes(odd, vel_out, heat_out, turb_out, mate_ref, cross_ref)
+
+
+def split_planes(odd, vel_ref, heat_ref, turb_ref, mate_ref, cross_ref):
+    rows = heat_ref.shape[1]
+    for f in range(6):
+        spot = slice(f * rows, (f + 1) * rows)
+        for ref, plane in ((mate_ref, 1 - odd), (cross_ref, odd)):
+            if f < 3:
+                ref[spot, :] = vel_ref[f, plane]
+            elif f == 3:
+                ref[spot, :] = heat_ref[plane]
+            else:
+                ref[spot, :] = turb_ref[f - 4, plane]
 
 
 def block_spot(index, rows, chunk, lanes):
@@ -302,7 +324,7 @@
         halo = HALO
     else:
         recv_ref, block_ref, mate_ref, cross_ref, pot_in, pot_out, send_ref = refs[:7]
-        wide_ref, turn_ref, flat_ref = refs[7:]
+        wide_ref, turn_ref = refs[7:]
         halo = HALO - SWEEPS
     window = chunk + 2 * halo
     place = lax.axis_index("slab")
@@ -364,12 +386,7 @@
                 c * window + SWEEPS : c * window + SWEEPS + keep
             ]
     else:
-        together = jnp.concatenate(own, 0)
-        lanes = ny * nz
-        for y in range(ny):
-            line = pltpu.roll(together, lanes - y * nz, 1) if y else together
-            flat_ref[pl.ds(y, 3 * chunk, stride=ny), :] = line[:, :LANES]
-        pot_out[...] = flat_ref[:, :nz]
+        pot_out[...] = jnp.concatenate(own, 0)
     mine = slice(halo, halo + chunk)
     conduct_own = conduct[mine]
     applied_own = [a[mine] for a in applied]
@@ -391,7 +408,8 @@
 def flow_kernel(last, *refs):
     vel_ref, heat_ref, turb_ref, mate_ref, cross_ref, recv_ref = refs[:6]
     if last:
-        vel_out, heat_out, turb_out, bordered_ref, loads_ref = refs[6:]
+        together_ref, vel_hbm, heat_hbm, turb_hbm, pot_hbm = refs[6:11]
+        bordered_ref, loads_ref, vel_out, heat_out, turb_out, pot_out, flat_ref, sems = refs[11:]
     else:
         labels_ref, table_ref = refs[6:8]
         vel_out, heat_out, turb_out, send_ref, mate_out, cross_out = refs[8:14]
@@ -400,6 +418,18 @@
     rows, wide = heat_ref.shape[1:]
     count, half, packed = recv_ref.shape
     chunk = packed // 8
+    moves = []
+    if last:
+        nz = pot_out.shape[1]
+        together = together_ref[...]
+        stacked, lanes = together.shape
+        ny = lanes // nz
+        for y in range(ny):
+            line = pltpu.roll(together, lanes - y * nz, 1) if y else together
+            flat_ref[pl.ds(y, stacked, stride=ny), :] = line[:, :LANES]
+        pot_out[...] = flat_ref[:, :nz]
+        moves.append(pltpu.make_async_copy(pot_out, pot_hbm, sems.at[0]))
+        moves[0].start()
     edge = jnp.zeros((8, wide), jnp.float32)
     for f in range(6):
         for plane in range(2):
@@ -494,27 +524,31 @@
                     for t in range(wide // LANES):
                         piece = part[:, t * LANES : (t + 1) * LANES]
                         sums_ref[t, spot, :] = piece if plane == 0 else sums_ref[t, spot, :] + piece
+        if last and (top + 8) % (rows // 2) == 0:
+            span = pl.ds(top + 8 - rows // 2, rows // 2)
+            for a, b in (
+                (vel_out.at[:, :, span], vel_hbm.at[:, :, span]),
+                (heat_out.at[:, span], heat_hbm.at[:, span]),
+                (turb_out.at[:, :, span], turb_hbm.at[:, :, span]),
+            ):
+                moves.append(pltpu.make_async_copy(a, b, sems.at[len(moves)]))
+                moves[-1].start()
     if last:
+        for move in moves:
+            move.wait()
         return
-    outs = [(vel_out, 0), (vel_out, 1), (vel_out, 2), (heat_out, None), (turb_out, 0), (turb_out, 1)]
-    for f, (ref, comp) in enumerate(outs):
-        if comp is None:
-            mate_out[f * rows : (f + 1) * rows, :] = ref[1 - odd]
-            cross_out[f * rows : (f + 1) * rows, :] = ref[odd]
-        else:
-            mate_out[f * rows : (f + 1) * rows, :] = ref[comp, 1 - odd]
-            cross_out[f * rows : (f + 1) * rows, :] = ref[comp, odd]
+    split_planes(odd, vel_out, heat_out, turb_out, mate_out, cross_out)
     pack_windows(sums_ref, labels_ref, table_ref, send_ref, HALO - SWEEPS)
 
 
-def call(kernel, outs, scratch, name, spaces, grant, cost, *operands):
+def call(kernel, outs, scratch, name, spaces, grant, cost, *operands, out_space=pltpu.VMEM):
     vmem = pl.BlockSpec(memory_space=pltpu.VMEM)
-    special = {"s": pl.BlockSpec(memory_space=pltpu.SMEM), "a": pl.BlockSpec(memory_space=pl.ANY)}
+    special = {"s": pl.BlockSpec(memory_space=pltpu.SMEM), "h": pl.BlockSpec(memory_space=pltpu.HBM)}
     return pl.pallas_call(
         kernel,
         out_shape=[jax.ShapeDtypeStruct(s, jnp.float32) for s in outs],
         in_specs=[special.get(spaces.get(i), vmem) for i in range(len(operands))],
-        out_specs=[vmem] * len(outs),
+        out_specs=[pl.BlockSpec(memory_space=out_space)] * len(outs),
         scratch_shapes=[pltpu.VMEM(s, jnp.float32) if isinstance(s, tuple) else s for s in scratch],
         name=name,
         cost_estimate=pl.CostEstimate(flops=cost, bytes_accessed=cost, transcendentals=0),
@@ -554,12 +588,15 @@
     joint = (6 * rows + 5 * chunk, wide)
     sums = (wide // LANES, 4 * rows, LANES)
     fields = (melt_speeds, heat_state, eddy_quantities)
-    mate, cross_side = call(
+    shapes = [a.shape for a in fields]
+    fields = [pltpu.with_memory_space_constraint(a, pltpu.HBM) for a in fields]
+    flat = [pltpu.with_memory_space_constraint(a, pltpu.HBM) for a in flat]
+    mate, cross_side, *fields = call(
         edge_kernel,
-        [joint, joint],
-        [(3 * chunk * ny, LANES), pltpu.SemaphoreType.DMA((12,))],
+        [joint, joint, *shapes],
+        [(3 * chunk * ny, LANES), (3, 3 * chunk * ny, nz), pltpu.SemaphoreType.DMA((6,))],
         "edges",
-        {0: "a", 1: "a", 2: "a"},
+        {i: "h" for i in range(6)},
         8,
         1 << 20,
         *fields,
@@ -577,22 +614,24 @@
         {3: "s"},
         8,
         1 << 22,
-        melt_speeds,
-        heat_state,
+        fields[0],
+        fields[1],
         zone_labels,
         zone_resistivity_inverse,
     )
     packed = (nz, ny // 2, 8 * chunk)
-    shapes = [a.shape for a in fields]
     for step_index in range(STEPS):
         first, last = step_index == 0, step_index == STEPS - 1
         arrived = lax.all_to_all(send, "slab", 0, 0, tiled=True)
+        if not first:
+            arrived, mate, cross_side = lax.optimization_barrier((arrived, mate, cross_side))
+            mate = lax.ppermute(mate, "slab", mates)
+            cross_side = lax.ppermute(cross_side, "slab", across)
         kept = () if first else (potential,)
         potential, loads = call(
             functools.partial(solve_kernel, chunk, ny, nz, rows, first),
-            [(3 * narrow, ny * nz) if first else (3 * chunk * ny, nz), packed],
-            [(2 if first else 1, ny * nz, LANES), (nz * ny // 2, LANES)]
-            + ([] if first else [(3 * chunk * ny, LANES)]),
+            [(3 * (narrow if first else chunk), ny * nz), packed],
+            [(2 if first else 1, ny * nz, LANES), (nz * ny // 2, LANES)],
             "sweeps",
             {},
             8,
@@ -608,8 +647,9 @@
         if last:
             fields = call(
                 functools.partial(flow_kernel, True),
-                shapes,
-                scratch,
+                [*shapes, flat[0].shape],
+                [*scratch, *shapes, flat[0].shape]
+                + [(3 * chunk * ny, LANES), pltpu.SemaphoreType.DMA((7,))],
                 "flow_last",
                 {},
                 12,
@@ -618,6 +658,8 @@
                 mate,
                 cross_side,
                 loads,
+                potential,
+                out_space=pltpu.HBM,
             )
         else:
             *fields, send, mate, cross_side = call(
@@ -635,8 +677,7 @@
                 zone_labels,
                 zone_resistivity_inverse,
             )
-            mate = lax.ppermute(mate, "slab", mates)
-            cross_side = lax.ppermute(cross_side, "slab", across)
+    *fields, potential = fields
     return (*fields, potential.reshape(imposed_induction.shape))
 
 

time: 74.1 us -> 66 us (0.89)
  local copies, waits for them, and re-layouts: 5.86 us -> 0.66 us
  blocking collectives: 49.2 us -> 47.2 us
    unnamed x22 -> x4, local copies, waits for them, and re-layouts: 5.86 us -> 0.66 us
    all_to_all x2, blocking collectives: 26.2 us -> 24.2 us  [window_plan(): arrived = lax.all_to_all(send, 'slab', 0, 0, tiled=True)]
  transfers between devices with their start and end apart: 4 -> 4, of which waited for: 0 -> 0; matrix products, arithmetic and copies ran while one was open for 0% -> 0% of each run, Pallas kernels for 5% -> 4%
where the time goes in v3:
time: 66 us; the launch traced here: 65.7 us
  blocking collectives  47.2 us (72%)
  Pallas kernels  11.4 us (17%)
  starting transfers between devices  5.76 us (9%)
  between operations  0.69 us (1%)
  local copies, waits for them, and re-layouts  0.66 us (1%)
    all_to_all x2, blocking collectives, window_plan(): arrived = lax.all_to_all(send, 'slab', 0, 0, tiled=True)  24.2 us
    all_to_all x2, blocking collectives, window_plan(): loads = lax.all_to_all(loads, 'slab', 0, 0, tiled=True)  23 us
    pallas_call x6, Pallas kernels, call(): pl.pallas_call(kernel, out_shape=[jax.ShapeDtypeStruct(s, jnp.float32) fo...  11.4 us
    ppermute x2, starting transfers between devices, window_plan(): mate = lax.ppermute(mate, 'slab', mates)  4.39 us
    ppermute x2, starting transfers between devices, window_plan(): cross_side = lax.ppermute(cross_side, 'slab', across)  1.37 us
  transfers between devices with their start and end apart: 4, of which 0 were waited for; matrix products, arithmetic and copies ran while one was open for 0% of the time, Pallas kernels for 4%

profile of v3, /device:TPU:0, one launch (start us, length us, event | category | flops | bytes accessed | tf_op | source)
XLA Modules:
  0.0 65.7 jit_solution(11439992082021786902)
XLA Ops:
  0.6 0.0 copy-start
  0.6 2.0 %edges.1 = (f32[272,512]{1,0:T(8,128)S(1)}, f32[272,512]{1,0:T(8,128)S(1)}, f32[3,2,32,512]{3,2,1,0:T(8,128)S(1)}, f32[2,32,512]{2,1,0:T(8,128)S(1)}, f32[2,2,32,512]{3,2,1,0:T(8,128)S(1)}) custom-call(f32[3,2,32,512]{3,2,1,0:T(8,128)} %vel_ref.1, f32[2,32,512]{2,1,0:T(8,128)} %heat_ref.1, f32[2,2,32,512]{3,2,1,0:T(8,128)} %turb_ref.1, f32[768,16]{1,0:T(8,128)} %bitcast.4, ...), custom_call_target="tpu_custom_call" | custom-call | flops 1048576 | bytes 1048576 | tf_op jit(solution)/shard_map/edges/pallas_call | solution.py:547
  2.6 0.7 %collective-permute-start.1 = (f32[272,512]{1,0:T(8,128)S(1)}, f32[272,512]{1,0:T(8,128)S(1)}, u32[]{:S(2)}, u32[]{:S(2)}) collective-permute-start(f32[272,512]{1,0:T(8,128)S(1)} %get-tuple-element.30), channel_id=1, source_target_pairs={{1,2},{3,4},{5,6},{7,8},{9,10},{11,12},{13,14},{2,1},{4,3},{6,5},{... | collective-permute-start | bytes 1671176 | tf_op jit(solution)/shard_map/ppermute | solution.py:607
  3.3 4.4 %collective-permute-start = (f32[272,512]{1,0:T(8,128)S(1)}, f32[272,512]{1,0:T(8,128)S(1)}, u32[]{:S(2)}, u32[]{:S(2)}) collective-permute-start(f32[272,512]{1,0:T(8,128)S(1)} %get-tuple-element.29.refs_1_), channel_id=1, source_target_pairs={{0,1},{1,0},{2,3},{3,2},{4,5},{5,4},{6,7},{7,6},{8,9},{9,8},{10,11... | collective-permute-start | bytes 1671176 | tf_op jit(solution)/shard_map/ppermute | solution.py:606
  7.7 0.0 copy-start.1
  7.7 0.0 copy-done
  7.7 0.7 copy-done.1
  8.4 1.1 %open_windows.1 = f32[16,24,128]{2,1,0:T(8,128)S(1)} custom-call(f32[3,2,32,512]{3,2,1,0:T(8,128)S(1)} %get-tuple-element.26.vel_ref.refs_0_, f32[2,32,512]{2,1,0:T(8,128)S(1)} %get-tuple-element.27.heat_ref.refs_1_, s32[1,16,256]{2,1,0:T(8,128)S(1)} %copy-done, f32[8]{0:T(128)S(1)} %copy-done.1), custom_call_target="tpu_custom_call" | custom-call | flops 4194304 | bytes 4194304 | tf_op jit(solution)/shard_map/open_windows/pallas_call | solution.py:547
  9.5 13.7 %all_to_all.20.refs_0_ = f32[16,24,128]{2,1,0:T(8,128)S(1)} all-to-all(f32[16,24,128]{2,1,0:T(8,128)S(1)} %open_windows.1), channel_id=1, replica_groups=mesh['groups'=2,'slab'=16] {'slab'}, dimensions={0} | all-to-all | bytes 393216 | tf_op jit(solution)/shard_map/all_to_all | solution.py:625
  23.2 0.0 collective-permute-done.1.refs_3_.refs_4_
  23.2 0.0 collective-permute-done.refs_2_.refs_3_
  23.2 2.0 %sweeps.2 = (f32[96,256]{1,0:T(8,128)S(1)}, f32[16,8,128]{2,1,0:T(8,128)S(1)}) custom-call(f32[16,24,128]{2,1,0:T(8,128)S(1)} %all_to_all.20.refs_0_, f32[272,512]{1,0:T(8,128)S(1)} %get-tuple-element.29.refs_1_, f32[272,512]{1,0:T(8,128)S(1)} %collective-permute-done.refs_2_.refs_3_, f32[272,512]{1,0:T(8,128)S(1)} %collective-permute-done.1.refs_3_.refs_4_), custom_call_target="tpu_custom_call" | custom-call | flops 4194304 | bytes 4194304 | tf_op jit(solution)/shard_map/sweeps/pallas_call | solution.py:547
  25.2 11.4 %all_to_all.21.refs_5_ = f32[16,8,128]{2,1,0:T(8,128)S(1)} all-to-all(f32[16,8,128]{2,1,0:T(8,128)S(1)} %get-tuple-element.31), channel_id=1, replica_groups=mesh['groups'=2,'slab'=16] {'slab'}, dimensions={0} | all-to-all | bytes 131072 | tf_op jit(solution)/shard_map/all_to_all | solution.py:645
  36.7 2.6 %flow_first.1 = (f32[3,2,32,512]{3,2,1,0:T(8,128)S(1)}, f32[2,32,512]{2,1,0:T(8,128)S(1)}, f32[2,2,32,512]{3,2,1,0:T(8,128)S(1)}, f32[16,16,128]{2,1,0:T(8,128)S...) custom-call(f32[3,2,32,512]{3,2,1,0:T(8,128)S(1)} %get-tuple-element.26.vel_ref.refs_0_, ...), custom_call_target="tpu_custom_call" | custom-call | flops 4194304 | bytes 4194304 | tf_op jit(solution)/shard_map/flow_first/pallas_call | solution.py:547
  39.3 10.5 %all_to_all.22.refs_0_ = f32[16,16,128]{2,1,0:T(8,128)S(1)} all-to-all(f32[16,16,128]{2,1,0:T(8,128)S(1)} %get-tuple-element.35), channel_id=1, replica_groups=mesh['groups'=2,'slab'=16] {'slab'}, dimensions={0} | all-to-all | bytes 262144 | tf_op jit(solution)/shard_map/all_to_all | solution.py:625
  49.8 0.0 collective-permute-start.2
  49.8 0.7 %collective-permute-start.3 = (f32[192,512]{1,0:T(8,128)S(1)}, f32[192,512]{1,0:T(8,128)S(1)}, u32[]{:S(2)}, u32[]{:S(2)}) collective-permute-start(f32[192,512]{1,0:T(8,128)S(1)} %get-tuple-element.39), channel_id=1, source_target_pairs={{1,2},{3,4},{5,6},{7,8},{9,10},{11,12},{13,14},{2,1},{4,3},{6,5},{... | collective-permute-start | bytes 1179656 | tf_op jit(solution)/shard_map/ppermute | solution.py:629
  50.4 1.4 %sweeps.3 = (f32[48,256]{1,0:T(8,128)S(1)}, f32[16,8,128]{2,1,0:T(8,128)S(1)}) custom-call(f32[16,16,128]{2,1,0:T(8,128)S(1)} %all_to_all.22.refs_0_, f32[272,512]{1,0:T(8,128)S(1)} %get-tuple-element.29.refs_1_, f32[272,512]{1,0:T(8,128)S(1)} %collective-permute-done.refs_2_.refs_3_, f32[272,512]{1,0:T(8,128)S(1)} %collective-permute-done.1.refs_3_.refs_4_, ...), custom_call_target="tpu_custom_call" | custom-call | flops 4194304 | bytes 4194304 | tf_op jit(solution)/shard_map/sweeps/pallas_call | solution.py:547
  51.9 11.5 %all_to_all.23.refs_5_ = f32[16,8,128]{2,1,0:T(8,128)S(1)} all-to-all(f32[16,8,128]{2,1,0:T(8,128)S(1)} %get-tuple-element.42), channel_id=1, replica_groups=mesh['groups'=2,'slab'=16] {'slab'}, dimensions={0} | all-to-all | bytes 131072 | tf_op jit(solution)/shard_map/all_to_all | solution.py:645
  63.4 0.0 collective-permute-done.2.refs_3_
  63.4 0.0 collective-permute-done.3.refs_4_
  63.4 2.3 %flow_last.1 = (f32[3,2,32,512]{3,2,1,0:T(8,128)}, f32[2,32,512]{2,1,0:T(8,128)}, f32[2,2,32,512]{3,2,1,0:T(8,128)}, f32[768,16]{1,0:T(8,128)}) custom-call(f32[3,2,32,512]{3,2,1,0:T(8,128)S(1)} %get-tuple-element.32.refs_0_, f32[2,32,512]{2,1,0:T(8,128)S(1)} %get-tuple-element.33.refs_1_, f32[2,2,32,512]{3,2,1,0:T(8,128)S(1)} %get-tuple-element.34.refs_2_, ...), custom_call_target="tpu_custom_call" | custom-call | flops 4194304 | bytes 4194304 | tf_op jit(solution)/shard_map/flow_last/pallas_call | solution.py:547
Async XLA Ops:
  0.6 7.1 %copy-start = (s32[1,16,256]{2,1,0:T(8,128)S(1)}, s32[1,16,256]{2,1,0:T(8,128)}, u32[]{:S(2)}) copy-start(s32[1,16,256]{2,1,0:T(8,128)} %refs_6_.1) | copy-start | bytes 49156
  2.6 20.6 %collective-permute-start.1 = (f32[272,512]{1,0:T(8,128)S(1)}, f32[272,512]{1,0:T(8,128)S(1)}, u32[]{:S(2)}, u32[]{:S(2)}) collective-permute-start(f32[272,512]{1,0:T(8,128)S(1)} %get-tuple-element.30), channel_id=1, source_target_pairs={{1,2},{3,4},{5,6},{7,8},{9,10},{11,12},{13,14},{2,1},{4,3},{6,5},{... | collective-permute-start | bytes 1671176 | tf_op jit(solution)/shard_map/ppermute | solution.py:607
  3.3 19.9 %collective-permute-start = (f32[272,512]{1,0:T(8,128)S(1)}, f32[272,512]{1,0:T(8,128)S(1)}, u32[]{:S(2)}, u32[]{:S(2)}) collective-permute-start(f32[272,512]{1,0:T(8,128)S(1)} %get-tuple-element.29.refs_1_), channel_id=1, source_target_pairs={{0,1},{1,0},{2,3},{3,2},{4,5},{5,4},{6,7},{7,6},{8,9},{9,8},{10,11... | collective-permute-start | bytes 1671176 | tf_op jit(solution)/shard_map/ppermute | solution.py:606
  7.7 0.7 copy-start.1
  49.8 13.6 %collective-permute-start.2 = (f32[192,512]{1,0:T(8,128)S(1)}, f32[192,512]{1,0:T(8,128)S(1)}, u32[]{:S(2)}, u32[]{:S(2)}) collective-permute-start(f32[192,512]{1,0:T(8,128)S(1)} %get-tuple-element.38), channel_id=1, source_target_pairs={{0,1},{1,0},{2,3},{3,2},{4,5},{5,4},{6,7},{7,6},{8,9},{9,8},{10,11... | collective-permute-start | bytes 1179656 | tf_op jit(solution)/shard_map/ppermute | solution.py:628
  49.8 13.6 %collective-permute-start.3 = (f32[192,512]{1,0:T(8,128)S(1)}, f32[192,512]{1,0:T(8,128)S(1)}, u32[]{:S(2)}, u32[]{:S(2)}) collective-permute-start(f32[192,512]{1,0:T(8,128)S(1)} %get-tuple-element.39), channel_id=1, source_target_pairs={{1,2},{3,4},{5,6},{7,8},{9,10},{11,12},{13,14},{2,1},{4,3},{6,5},{... | collective-permute-start | bytes 1179656 | tf_op jit(solution)/shard_map/ppermute | solution.py:629

commit v4 on v3

--- a/solution.py
+++ b/solution.py
@@ -6,6 +6,7 @@
 from jax.experimental import pallas as pl
 from jax.experimental.pallas import tpu as pltpu
 from jax.sharding import PartitionSpec as P
+
 
 STEPS = 2
 SWEEPS = 8
@@ -93,7 +94,7 @@
     motional = cross(coupled[:3], imposed_induction)
     source = conduct * motional + winding_current
     diagonal = 6.0 + coupling * conduct
-    for sweep_index in range(SWEEPS):
+    for _ in range(SWEEPS):
         potential = (source + neighbours(faces(potential))) / diagonal
     drive_field = motional - coupling * potential
     current = conduct * drive_field + winding_current
@@ -175,7 +176,7 @@
     potential = jnp.transpose(arrived[0], (0, 3, 2, 1))
     field_local = jnp.transpose(arrived[1], (0, 3, 2, 1))
     coil_local = jnp.transpose(arrived[2], (0, 3, 2, 1))
-    for step_index in range(STEPS):
+    for _ in range(STEPS):
         coupled = local_coupled(induction_tables, zone_labels, zone_resistivity_inverse)
         potential, em_loads = relax(coupled, field_local, coil_local, potential)
         induction_tables = flow_step(induction_tables, prolong(em_loads))
@@ -209,10 +210,10 @@
     return jnp.where(picked, jnp.float32(weight), jnp.float32(0.0)).astype(jnp.bfloat16)
 
 
-def pack_windows(sums_ref, labels_ref, table_ref, send_ref, halo):
+def pack_windows(sums_ref, admit_ref, send_ref, halo):
     tiles, rows, _ = sums_ref.shape
     wide = tiles * LANES
-    count, ny = send_ref.shape[0], labels_ref.shape[1]
+    count, ny = send_ref.shape[0], admit_ref.shape[0]
     paired = jnp.concatenate(
         [
             sums_ref[t, pl.ds(0, rows // 2, stride=2), :] + sums_ref[t, pl.ds(1, rows // 2, stride=2), :]
@@ -221,11 +222,7 @@
         1,
     )
     coarse = exact_dot(paired, pair_chooser(wide, 0.125, False))
-    labels = labels_ref[0]
-    admittance = jnp.zeros(labels.shape, jnp.float32)
-    for region in range(table_ref.shape[0]):
-        admittance = jnp.where(labels == region, table_ref[region], admittance)
-    coupled = jnp.concatenate([coarse[: 3 * ny], coarse[3 * ny :] * admittance], 0)
+    coupled = jnp.concatenate([coarse[: 3 * ny], coarse[3 * ny :] * admit_ref[...]], 0)
     nx = wide // 2
     chunk = nx // count
     window = chunk + 2 * halo
@@ -251,26 +248,32 @@
     guess_ref,
     applied_ref,
     coil_ref,
+    labels_ref,
+    table_ref,
+    block_ref,
     mate_ref,
     cross_ref,
+    admit_ref,
     vel_out,
     heat_out,
     turb_out,
     flat_ref,
     raw_ref,
+    zones_ref,
+    known_ref,
     sems,
 ):
     odd = lax.rem(lax.axis_index("slab"), 2)
-    rows = heat_ref.shape[1]
     pairs = [(guess_ref, raw_ref.at[0]), (applied_ref, raw_ref.at[1]), (coil_ref, raw_ref.at[2])]
     pairs += [(vel_ref, vel_out), (heat_ref, heat_out), (turb_ref, turb_out)]
+    pairs += [(labels_ref, zones_ref), (table_ref, known_ref)]
     moves = [pltpu.make_async_copy(a, b, sems.at[i]) for i, (a, b) in enumerate(pairs)]
     for move in moves:
         move.start()
     for move in moves[:3]:
         move.wait()
     total, nz = guess_ref.shape
-    chunk = (mate_ref.shape[0] - 6 * rows) // 5
+    chunk = block_ref.shape[0] // 5
     ny = total // (3 * chunk)
     lanes = ny * nz
     for kind in range(3):
@@ -279,13 +282,15 @@
     for kind in range(3):
         packed = jnp.concatenate([line[:, kind * nz : (kind + 1) * nz] for line in lines], 1)
         for c in range(3):
-            row, lane = block_spot(3 * kind + c, rows, chunk, lanes)
-            piece = packed[c * chunk : (c + 1) * chunk]
-            mate_ref[row, lane] = piece
-            cross_ref[row, lane] = piece
+            block_ref[block_spot(3 * kind + c, chunk, lanes)] = packed[c * chunk : (c + 1) * chunk]
     for move in moves[3:]:
         move.wait()
     split_planes(odd, vel_out, heat_out, turb_out, mate_ref, cross_ref)
+    labels = zones_ref[0]
+    admittance = jnp.zeros(labels.shape, jnp.float32)
+    for region in range(table_ref.shape[0]):
+        admittance = jnp.where(labels == region, known_ref[region], admittance)
+    admit_ref[...] = admittance
 
 
 def split_planes(odd, vel_ref, heat_ref, turb_ref, mate_ref, cross_ref):
@@ -301,12 +306,12 @@
                 ref[spot, :] = turb_ref[f - 4, plane]
 
 
-def block_spot(index, rows, chunk, lanes):
-    row = 6 * rows + (index % 5) * chunk
-    return slice(row, row + chunk), slice(index // 5 * lanes, (index // 5 + 1) * lanes)
-
-
-def open_kernel(vel_ref, heat_ref, labels_ref, table_ref, send_ref, sums_ref):
+def block_spot(index, chunk, lanes):
+    row, lane = index % 5 * chunk, index // 5 * lanes
+    return slice(row, row + chunk), slice(lane, lane + lanes)
+
+
+def open_kernel(vel_ref, heat_ref, admit_ref, send_ref, sums_ref):
     rows = heat_ref.shape[1]
     for t in range(sums_ref.shape[0]):
         at = slice(t * LANES, (t + 1) * LANES)
@@ -315,16 +320,15 @@
         sums_ref[t, 3 * rows :, :] = jnp.exp(
             -thermal_gradient_factor * heat_ref[0, :, at]
         ) + jnp.exp(-thermal_gradient_factor * heat_ref[1, :, at])
-    pack_windows(sums_ref, labels_ref, table_ref, send_ref, HALO)
-
-
-def solve_kernel(chunk, ny, nz, rows, first, *refs):
+    pack_windows(sums_ref, admit_ref, send_ref, HALO)
+
+
+def solve_kernel(chunk, ny, nz, first, *refs):
     if first:
-        recv_ref, block_ref, mate_ref, cross_ref, pot_out, send_ref, wide_ref, turn_ref = refs
+        recv_ref, block_ref, mate_ref, cross_ref, kept_ref, send_ref, wide_ref, turn_ref = refs
         halo = HALO
     else:
-        recv_ref, block_ref, mate_ref, cross_ref, pot_in, pot_out, send_ref = refs[:7]
-        wide_ref, turn_ref = refs[7:]
+        recv_ref, held_ref, pot_out, send_ref, wide_ref, turn_ref = refs
         halo = HALO - SWEEPS
     window = chunk + 2 * halo
     place = lax.axis_index("slab")
@@ -344,19 +348,23 @@
     def windowed(kind):
         found = []
         for c in range(3):
-            row, lane = block_spot(3 * kind + c, rows, chunk, ny * nz)
-            mate, cross_side = mate_ref[row, lane], cross_ref[row, lane]
+            if not first:
+                at = (3 * kind + c) * window
+                found.append(held_ref[at : at + window, :])
+                continue
+            spot = block_spot(3 * kind + c, chunk, ny * nz)
+            mate, cross_side = mate_ref[spot], cross_ref[spot]
             low = jnp.where(odd == 0, cross_side, mate)
             high = jnp.where(odd == 0, mate, cross_side)
             found.append(
                 jnp.concatenate(
-                    [low[chunk - halo :], block_ref[row, lane], high[:halo]], 0
+                    [low[chunk - halo :], block_ref[spot], high[:halo]], 0
                 )
             )
         return found
 
     applied, coil = windowed(1), windowed(2)
-    potential = jnp.concatenate(windowed(0), 0) if first else pot_in[...]
+    potential = jnp.concatenate(windowed(0), 0)
     motional = [
         velocity[1] * applied[2] - velocity[2] * applied[1],
         velocity[2] * applied[0] - velocity[0] * applied[2],
@@ -371,7 +379,7 @@
     shape = potential.shape
     lane = lax.broadcasted_iota(jnp.int32, shape, 1)
     column = lax.rem(lane, nz)
-    for sweep in range(SWEEPS):
+    for _ in range(SWEEPS):
         around = pltpu.roll(potential, 1, 0) + pltpu.roll(potential, shape[0] - 1, 0)
         around += jnp.where(column == 0, 0.0, pltpu.roll(potential, 1, 1))
         around += jnp.where(column == nz - 1, 0.0, pltpu.roll(potential, shape[1] - 1, 1))
@@ -381,10 +389,9 @@
     own = [potential[c * window + halo : c * window + halo + chunk] for c in range(3)]
     if first:
         keep = chunk + 2 * (halo - SWEEPS)
-        for c in range(3):
-            pot_out[c * keep : (c + 1) * keep, :] = potential[
-                c * window + SWEEPS : c * window + SWEEPS + keep
-            ]
+        whole = [potential[c * window : (c + 1) * window] for c in range(3)] + applied + coil
+        for i, array in enumerate(whole):
+            kept_ref[i * keep : (i + 1) * keep, :] = array[SWEEPS : SWEEPS + keep]
     else:
         pot_out[...] = jnp.concatenate(own, 0)
     mine = slice(halo, halo + chunk)
@@ -411,12 +418,12 @@
         together_ref, vel_hbm, heat_hbm, turb_hbm, pot_hbm = refs[6:11]
         bordered_ref, loads_ref, vel_out, heat_out, turb_out, pot_out, flat_ref, sems = refs[11:]
     else:
-        labels_ref, table_ref = refs[6:8]
-        vel_out, heat_out, turb_out, send_ref, mate_out, cross_out = refs[8:14]
-        bordered_ref, loads_ref, sums_ref = refs[14:]
+        admit_ref = refs[6]
+        vel_out, heat_out, turb_out, send_ref, mate_out, cross_out = refs[7:13]
+        bordered_ref, loads_ref, sums_ref = refs[13:]
     odd = lax.rem(lax.axis_index("slab"), 2)
     rows, wide = heat_ref.shape[1:]
-    count, half, packed = recv_ref.shape
+    count, _, packed = recv_ref.shape
     chunk = packed // 8
     moves = []
     if last:
@@ -538,30 +545,31 @@
             move.wait()
         return
     split_planes(odd, vel_out, heat_out, turb_out, mate_out, cross_out)
-    pack_windows(sums_ref, labels_ref, table_ref, send_ref, HALO - SWEEPS)
-
-
-def call(kernel, outs, scratch, name, spaces, grant, cost, *operands, out_space=pltpu.VMEM):
+    pack_windows(sums_ref, admit_ref, send_ref, HALO - SWEEPS)
+
+
+def call(kernel, outs, scratch, spaces, grant, cost, *operands, out_space=None):
     vmem = pl.BlockSpec(memory_space=pltpu.VMEM)
     special = {"s": pl.BlockSpec(memory_space=pltpu.SMEM), "h": pl.BlockSpec(memory_space=pltpu.HBM)}
     return pl.pallas_call(
         kernel,
         out_shape=[jax.ShapeDtypeStruct(s, jnp.float32) for s in outs],
         in_specs=[special.get(spaces.get(i), vmem) for i in range(len(operands))],
-        out_specs=[pl.BlockSpec(memory_space=out_space)] * len(outs),
+        out_specs=[pl.BlockSpec(memory_space=m) for m in out_space or [pltpu.VMEM] * len(outs)],
         scratch_shapes=[pltpu.VMEM(s, jnp.float32) if isinstance(s, tuple) else s for s in scratch],
-        name=name,
         cost_estimate=pl.CostEstimate(flops=cost, bytes_accessed=cost, transcendentals=0),
         compiler_params=pltpu.CompilerParams(vmem_limit_bytes=grant << 20),
     )(*operands)
 
 
-def beside(block):
+def trade(mate, cross_side):
     count = lax.axis_size("slab")
     mates = [(i, i ^ 1) for i in range(count)]
     across = [(i, i + 1) for i in range(1, count - 1, 2)]
     across = across + [(b, a) for a, b in across]
-    return mates, across
+    cross_side = lax.ppermute(cross_side, "slab", across)
+    mate = lax.ppermute(mate, "slab", mates)
+    return mate, cross_side
 
 
 def window_plan(
@@ -577,7 +585,6 @@
     count = lax.axis_size("slab")
     _, chunk, ny, nz = imposed_induction.shape
     _, rows, wide = heat_state.shape
-    mates, across = beside(None)
     flat = [
         a.reshape(3 * chunk * ny, nz)
         for a in (window_entry_induction_guess, imposed_induction, winding_current)
@@ -585,63 +592,55 @@
     window, narrow = chunk + 2 * HALO, chunk + 2 * (HALO - SWEEPS)
     tall = ny + ny // 2 if 4 * window > LANES else ny
     edge = (6 * rows, wide)
-    joint = (6 * rows + 5 * chunk, wide)
     sums = (wide // LANES, 4 * rows, LANES)
     fields = (melt_speeds, heat_state, eddy_quantities)
     shapes = [a.shape for a in fields]
-    fields = [pltpu.with_memory_space_constraint(a, pltpu.HBM) for a in fields]
-    flat = [pltpu.with_memory_space_constraint(a, pltpu.HBM) for a in flat]
-    mate, cross_side, *fields = call(
+    raw = [*fields, *flat, zone_labels, zone_resistivity_inverse]
+    raw = [pltpu.with_memory_space_constraint(a, pltpu.HBM) for a in raw]
+    block, mate, cross_side, admittance, *fields = call(
         edge_kernel,
-        [joint, joint, *shapes],
-        [(3 * chunk * ny, LANES), (3, 3 * chunk * ny, nz), pltpu.SemaphoreType.DMA((6,))],
-        "edges",
-        {i: "h" for i in range(6)},
+        [(5 * chunk, wide), edge, edge, zone_labels.shape[1:], *shapes],
+        [
+            (3 * chunk * ny, LANES),
+            (3, 3 * chunk * ny, nz),
+            pltpu.VMEM(zone_labels.shape, jnp.int32),
+            pltpu.SMEM(zone_resistivity_inverse.shape, jnp.float32),
+            pltpu.SemaphoreType.DMA((len(raw),)),
+        ],
+        {i: "h" for i in range(len(raw))},
         8,
         1 << 20,
-        *fields,
-        *flat,
-    )
-    block = mate
-    mate = lax.ppermute(mate, "slab", mates)
-    cross_side = lax.ppermute(cross_side, "slab", across)
-    block_mate, block_cross = mate, cross_side
+        *raw,
+    )
     (send,) = call(
         open_kernel,
         [(count, tall, LANES)],
         [sums],
-        "open_windows",
-        {3: "s"},
+        {},
         8,
         1 << 22,
         fields[0],
         fields[1],
-        zone_labels,
-        zone_resistivity_inverse,
+        admittance,
     )
     packed = (nz, ny // 2, 8 * chunk)
     for step_index in range(STEPS):
         first, last = step_index == 0, step_index == STEPS - 1
         arrived = lax.all_to_all(send, "slab", 0, 0, tiled=True)
-        if not first:
-            arrived, mate, cross_side = lax.optimization_barrier((arrived, mate, cross_side))
-            mate = lax.ppermute(mate, "slab", mates)
-            cross_side = lax.ppermute(cross_side, "slab", across)
-        kept = () if first else (potential,)
+        if first:
+            held = (block, *trade(block, block))
+        mate, cross_side = trade(mate, cross_side)
         potential, loads = call(
-            functools.partial(solve_kernel, chunk, ny, nz, rows, first),
-            [(3 * (narrow if first else chunk), ny * nz), packed],
+            functools.partial(solve_kernel, chunk, ny, nz, first),
+            [(9 * narrow if first else 3 * chunk, ny * nz), packed],
             [(2 if first else 1, ny * nz, LANES), (nz * ny // 2, LANES)],
-            "sweeps",
             {},
             8,
             1 << 22,
             arrived,
-            block,
-            block_mate,
-            block_cross,
-            *kept,
+            *held,
         )
+        held = (potential,)
         loads = lax.all_to_all(loads, "slab", 0, 0, tiled=True)
         scratch = [(6, 2, rows + 16, wide), sums]
         if last:
@@ -650,7 +649,6 @@
                 [*shapes, flat[0].shape],
                 [*scratch, *shapes, flat[0].shape]
                 + [(3 * chunk * ny, LANES), pltpu.SemaphoreType.DMA((7,))],
-                "flow_last",
                 {},
                 12,
                 1 << 22,
@@ -659,23 +657,21 @@
                 cross_side,
                 loads,
                 potential,
-                out_space=pltpu.HBM,
+                out_space=[pltpu.HBM] * 4,
             )
         else:
             *fields, send, mate, cross_side = call(
                 functools.partial(flow_kernel, False),
                 shapes + [(count, ny, LANES), edge, edge],
                 scratch + [sums],
-                "flow_first",
-                {7: "s"},
+                {},
                 12,
                 1 << 22,
                 *fields,
                 mate,
                 cross_side,
                 loads,
-                zone_labels,
-                zone_resistivity_inverse,
+                admittance,
             )
     *fields, potential = fields
     return (*fields, potential.reshape(imposed_induction.shape))
@@ -684,7 +680,7 @@
 def on_device(*arrays):
     count = lax.axis_size("slab")
     _, chunk, ny, nz = arrays[5].shape
-    planes, rows, wide = arrays[1].shape
+    planes, _, wide = arrays[1].shape
     narrow = chunk + 2 * (HALO - SWEEPS)
     fits = (
         STEPS == 2

time: 66 us -> 73.4 us (1.11)
  blocking collectives: 47.2 us -> 23.2 us
  starting transfers between devices: 5.76 us -> 27.8 us
  waiting for transfers between devices: 0.01 us -> 9.64 us
    all_to_all x0 -> x2, starting transfers between devices: none -> 20.9 us  [the longest x1 13.5 us: window_plan(): loads = lax.all_to_all(loads, 'slab', 0, 0, tiled=True)]
    all_to_all x2 -> x1, blocking collectives: 23 us -> 10.8 us  [window_plan(): loads = lax.all_to_all(loads, 'slab', 0, 0, tiled=True)]
    all_to_all x2 -> x1, blocking collectives: 24.2 us -> 12.4 us  [window_plan(): arrived = lax.all_to_all(send, 'slab', 0, 0, tiled=True)]
    all_to_all x0 -> x2, waiting for transfers between devices: none -> 8.6 us  [the longest x1 6.88 us: window_plan(): loads = lax.all_to_all(loads, 'slab', 0, 0, tiled=True)]
    ppermute x4 -> x6, starting transfers between devices: 5.76 us -> 6.95 us  [the longest x3 4.92 us: trade(): mate = lax.ppermute(mate, 'slab', mates)]
    ppermute x4 -> x6, waiting for transfers between devices: 0.01 us -> 1.04 us  [the longest x3 1.03 us: trade(): mate = lax.ppermute(mate, 'slab', mates)]
  transfers between devices with their start and end apart: 4 -> 8, of which waited for: 0 -> 3; matrix products, arithmetic and copies ran while one was open for 0% -> 0% of each run, Pallas kernels for 4% -> 6%
where the time goes in v4:
time: 73.4 us; the launch traced here: 73 us
  starting transfers between devices  27.8 us (38%)
  blocking collectives  23.2 us (32%)
  Pallas kernels  11.6 us (16%)
  waiting for transfers between devices  9.64 us (13%)
    all_to_all x1, starting transfers between devices, window_plan(): loads = lax.all_to_all(loads, 'slab', 0, 0, tiled=True)  13.5 us
    all_to_all x1, blocking collectives, window_plan(): arrived = lax.all_to_all(send, 'slab', 0, 0, tiled=True)  12.4 us
    pallas_call x6, Pallas kernels, call(): pl.pallas_call(kernel, out_shape=[jax.ShapeDtypeStruct(s, jnp.float32) fo...  11.6 us
    all_to_all x1, blocking collectives, window_plan(): loads = lax.all_to_all(loads, 'slab', 0, 0, tiled=True)  10.8 us
    all_to_all x1, starting transfers between devices, window_plan(): arrived = lax.all_to_all(send, 'slab', 0, 0, tiled=True)  7.41 us
    all_to_all x1, waiting for transfers between devices, window_plan(): loads = lax.all_to_all(loads, 'slab', 0, 0, tiled=True)  6.88 us
    ppermute x3, starting transfers between devices, trade(): mate = lax.ppermute(mate, 'slab', mates)  4.92 us
    ppermute x3, starting transfers between devices, trade(): cross_side = lax.ppermute(cross_side, 'slab', across)  2.03 us
  transfers between devices with their start and end apart: 8, of which 3 were waited for; matrix products, arithmetic and copies ran while one was open for 0% of the time, Pallas kernels for 6%

profile of v4, /device:TPU:0, one launch (start us, length us, event | category | flops | bytes accessed | tf_op | source)
XLA Modules:
  0.0 73.0 jit_solution(4275075920459054968)
XLA Ops:
  0.6 2.0 %shard_map.111 = (f32[80,512]{1,0:T(8,128)S(1)}, f32[192,512]{1,0:T(8,128)S(1)}, f32[192,512]{1,0:T(8,128)S(1)}, f32[16,256]{1,0:T(8,128)S(1)}, f32[3,2,32,512]{...) custom-call(f32[3,2,32,512]{3,2,1,0:T(8,128)} %vel_ref.1, f32[2,32,512]{2,1,0:T(8,128)} %heat_ref.1, ...), custom_call_target="tpu_custom_call" | custom-call | flops 1048576 | bytes 1048576 | tf_op jit(solution)/shard_map/pallas_call | solution.py:554
  2.7 1.2 %shard_map.112 = f32[16,24,128]{2,1,0:T(8,128)} custom-call(f32[3,2,32,512]{3,2,1,0:T(8,128)S(1)} %get-tuple-element.25.vel_ref.refs_0_, f32[2,32,512]{2,1,0:T(8,128)S(1)} %get-tuple-element.26.heat_ref.refs_1_, f32[16,256]{1,0:T(8,128)S(1)} %get-tuple-element.30.admit_ref.refs_6_), custom_call_target="tpu_custom_call" | custom-call | flops 4194304 | bytes 4194304 | tf_op jit(solution)/shard_map/pallas_call | solution.py:554
  3.9 7.4 %all-to-all-start = ((f32[16,24,128]{2,1,0:T(8,128)}), f32[16,24,128]{2,1,0:T(8,128)S(1)}, u32[]{:S(2)}, u32[]{:S(2)}) async-start(f32[16,24,128]{2,1,0:T(8,128)} %shard_map.112), calls=%async_computation | async-start | bytes 393216 | tf_op jit(solution)/shard_map/all_to_all | solution.py:629
  11.3 0.4 collective-permute-start
  11.7 0.7 collective-permute-start.1
  12.4 0.7 collective-permute-start.3
  13.1 4.4 %collective-permute-start.2 = (f32[80,512]{1,0:T(8,128)S(1)}, f32[80,512]{1,0:T(8,128)S(1)}, u32[]{:S(2)}, u32[]{:S(2)}) collective-permute-start(f32[80,512]{1,0:T(8,128)S(1)} %get-tuple-element.31.refs_1_), channel_id=1, source_target_pairs={{0,1},{1,0},{2,3},{3,2},{4,5},{5,4},{6,7},{7,6},{8,9},{9,8},{10,11... | collective-permute-start | bytes 491528 | tf_op jit(solution)/shard_map/ppermute | solution.py:571
  17.5 0.0 collective-permute-done.3.refs_3_
  17.5 1.0 %collective-permute-done.2.refs_2_ = f32[80,512]{1,0:T(8,128)S(1)} collective-permute-done((f32[80,512]{1,0:T(8,128)S(1)}, f32[80,512]{1,0:T(8,128)S(1)}, u32[]{:S(2)}, u32[]{:S(2)}) %collective-permute-start.2) | collective-permute-done | bytes 163872 | tf_op jit(solution)/shard_map/ppermute | solution.py:571
  18.6 1.7 %all-to-all-done.refs_0_ = f32[16,24,128]{2,1,0:T(8,128)S(1)} async-done(((f32[16,24,128]{2,1,0:T(8,128)}), f32[16,24,128]{2,1,0:T(8,128)S(1)}, u32[]{:S(2)}, u32[]{:S(2)}) %all-to-all-start) | async-done | bytes 196640 | tf_op jit(solution)/shard_map/all_to_all | solution.py:629
  20.3 2.6 %shard_map.113 = (f32[288,256]{1,0:T(8,128)S(1)}, f32[16,8,128]{2,1,0:T(8,128)}) custom-call(f32[16,24,128]{2,1,0:T(8,128)S(1)} %all-to-all-done.refs_0_, f32[80,512]{1,0:T(8,128)S(1)} %get-tuple-element.31.refs_1_, f32[80,512]{1,0:T(8,128)S(1)} %collective-permute-done.2.refs_2_, f32[80,512]{1,0:T(8,128)S(1)} %collective-permute-done.3.refs_3_), custom_call_target="tpu_custom_call" | custom-call | flops 4194304 | bytes 4194304 | tf_op jit(solution)/shard_map/pallas_call | solution.py:554
  22.9 13.5 %all-to-all-start.1 = ((f32[16,8,128]{2,1,0:T(8,128)}), f32[16,8,128]{2,1,0:T(8,128)S(1)}, u32[]{:S(2)}, u32[]{:S(2)}) async-start(f32[16,8,128]{2,1,0:T(8,128)} %get-tuple-element.32), calls=%async_computation.1 | async-start | bytes 131072 | tf_op jit(solution)/shard_map/all_to_all | solution.py:644
  36.4 0.0 collective-permute-done.refs_3_
  36.4 0.0 collective-permute-done.1.refs_4_
  36.4 6.9 %all-to-all-done.1.refs_5_ = f32[16,8,128]{2,1,0:T(8,128)S(1)} async-done(((f32[16,8,128]{2,1,0:T(8,128)}), f32[16,8,128]{2,1,0:T(8,128)S(1)}, u32[]{:S(2)}, u32[]{:S(2)}) %all-to-all-start.1) | async-done | bytes 65568 | tf_op jit(solution)/shard_map/all_to_all | solution.py:644
  43.3 2.0 %shard_map.114 = (f32[3,2,32,512]{3,2,1,0:T(8,128)S(1)}, f32[2,32,512]{2,1,0:T(8,128)S(1)}, f32[2,2,32,512]{3,2,1,0:T(8,128)S(1)}, f32[16,16,128]{2,1,0:T(8,128)...) custom-call(f32[3,2,32,512]{3,2,1,0:T(8,128)S(1)} %get-tuple-element.25.vel_ref.refs_0_, ...), custom_call_target="tpu_custom_call" | custom-call | flops 4194304 | bytes 4194304 | tf_op jit(solution)/shard_map/pallas_call | solution.py:554
  45.3 0.1 collective-permute-start.4
  45.4 0.7 collective-permute-start.5
  46.1 12.4 %all_to_all.20.refs_0_ = f32[16,16,128]{2,1,0:T(8,128)S(1)} all-to-all(f32[16,16,128]{2,1,0:T(8,128)S(1)} %get-tuple-element.38), channel_id=1, replica_groups=mesh['groups'=2,'slab'=16] {'slab'}, dimensions={0} | all-to-all | bytes 262144 | tf_op jit(solution)/shard_map/all_to_all | solution.py:629
  58.5 1.4 %shard_map.115 = (f32[48,256]{1,0:T(8,128)S(1)}, f32[16,8,128]{2,1,0:T(8,128)S(1)}) custom-call(f32[16,16,128]{2,1,0:T(8,128)S(1)} %all_to_all.20.refs_0_, f32[288,256]{1,0:T(8,128)S(1)} %get-tuple-element.39.refs_1_), custom_call_target="tpu_custom_call" | custom-call | flops 4194304 | bytes 4194304 | tf_op jit(solution)/shard_map/pallas_call | solution.py:554
  59.9 10.8 %all_to_all.21.refs_5_ = f32[16,8,128]{2,1,0:T(8,128)S(1)} all-to-all(f32[16,8,128]{2,1,0:T(8,128)S(1)} %get-tuple-element.40), channel_id=1, replica_groups=mesh['groups'=2,'slab'=16] {'slab'}, dimensions={0} | all-to-all | bytes 131072 | tf_op jit(solution)/shard_map/all_to_all | solution.py:644
  70.7 0.0 collective-permute-done.4.refs_3_
  70.7 0.0 collective-permute-done.5.refs_4_
  70.7 2.3 %shard_map.116 = (f32[3,2,32,512]{3,2,1,0:T(8,128)}, f32[2,32,512]{2,1,0:T(8,128)}, f32[2,2,32,512]{3,2,1,0:T(8,128)}, f32[768,16]{1,0:T(8,128)}) custom-call(f32[3,2,32,512]{3,2,1,0:T(8,128)S(1)} %get-tuple-element.33.refs_0_, f32[2,32,512]{2,1,0:T(8,128)S(1)} %get-tuple-element.34.refs_1_, f32[2,2,32,512]{3,2,1,0:T(8,128)S(1)} %get-tuple-element.35.refs_2_, ...), custom_call_target="tpu_custom_call" | custom-call | flops 4194304 | bytes 4194304 | tf_op jit(solution)/shard_map/pallas_call | solution.py:554
Async XLA Ops:
  3.9 16.4 %all-to-all-start = ((f32[16,24,128]{2,1,0:T(8,128)}), f32[16,24,128]{2,1,0:T(8,128)S(1)}, u32[]{:S(2)}, u32[]{:S(2)}) async-start(f32[16,24,128]{2,1,0:T(8,128)} %shard_map.112), calls=%async_computation | async-start | bytes 393216 | tf_op jit(solution)/shard_map/all_to_all | solution.py:629
  11.3 25.1 %collective-permute-start = (f32[192,512]{1,0:T(8,128)S(1)}, f32[192,512]{1,0:T(8,128)S(1)}, u32[]{:S(2)}, u32[]{:S(2)}) collective-permute-start(f32[192,512]{1,0:T(8,128)S(1)} %get-tuple-element.28), channel_id=1, source_target_pairs={{0,1},{1,0},{2,3},{3,2},{4,5},{5,4},{6,7},{7,6},{8,9},{9,8},{10,11... | collective-permute-start | bytes 1179656 | tf_op jit(solution)/shard_map/ppermute | solution.py:571
  11.7 24.7 %collective-permute-start.1 = (f32[192,512]{1,0:T(8,128)S(1)}, f32[192,512]{1,0:T(8,128)S(1)}, u32[]{:S(2)}, u32[]{:S(2)}) collective-permute-start(f32[192,512]{1,0:T(8,128)S(1)} %get-tuple-element.29), channel_id=1, source_target_pairs={{1,2},{3,4},{5,6},{7,8},{9,10},{11,12},{13,14},{2,1},{4,3},{6,5},{... | collective-permute-start | bytes 1179656 | tf_op jit(solution)/shard_map/ppermute | solution.py:570
  12.4 5.1 %collective-permute-start.3 = (f32[80,512]{1,0:T(8,128)S(1)}, f32[80,512]{1,0:T(8,128)S(1)}, u32[]{:S(2)}, u32[]{:S(2)}) collective-permute-start(f32[80,512]{1,0:T(8,128)S(1)} %get-tuple-element.31.refs_1_), channel_id=1, source_target_pairs={{1,2},{3,4},{5,6},{7,8},{9,10},{11,12},{13,14},{2,1},{4,3},{6,5},{... | collective-permute-start | bytes 491528 | tf_op jit(solution)/shard_map/ppermute | solution.py:570
  13.1 5.5 %collective-permute-start.2 = (f32[80,512]{1,0:T(8,128)S(1)}, f32[80,512]{1,0:T(8,128)S(1)}, u32[]{:S(2)}, u32[]{:S(2)}) collective-permute-start(f32[80,512]{1,0:T(8,128)S(1)} %get-tuple-element.31.refs_1_), channel_id=1, source_target_pairs={{0,1},{1,0},{2,3},{3,2},{4,5},{5,4},{6,7},{7,6},{8,9},{9,8},{10,11... | collective-permute-start | bytes 491528 | tf_op jit(solution)/shard_map/ppermute | solution.py:571
  22.9 20.4 %all-to-all-start.1 = ((f32[16,8,128]{2,1,0:T(8,128)}), f32[16,8,128]{2,1,0:T(8,128)S(1)}, u32[]{:S(2)}, u32[]{:S(2)}) async-start(f32[16,8,128]{2,1,0:T(8,128)} %get-tuple-element.32), calls=%async_computation.1 | async-start | bytes 131072 | tf_op jit(solution)/shard_map/all_to_all | solution.py:644
  45.3 25.4 %collective-permute-start.4 = (f32[192,512]{1,0:T(8,128)S(1)}, f32[192,512]{1,0:T(8,128)S(1)}, u32[]{:S(2)}, u32[]{:S(2)}) collective-permute-start(f32[192,512]{1,0:T(8,128)S(1)} %get-tuple-element.36), channel_id=1, source_target_pairs={{0,1},{1,0},{2,3},{3,2},{4,5},{5,4},{6,7},{7,6},{8,9},{9,8},{10,11... | collective-permute-start | bytes 1179656 | tf_op jit(solution)/shard_map/ppermute | solution.py:571
  45.4 25.3 %collective-permute-start.5 = (f32[192,512]{1,0:T(8,128)S(1)}, f32[192,512]{1,0:T(8,128)S(1)}, u32[]{:S(2)}, u32[]{:S(2)}) collective-permute-start(f32[192,512]{1,0:T(8,128)S(1)} %get-tuple-element.37), channel_id=1, source_target_pairs={{1,2},{3,4},{5,6},{7,8},{9,10},{11,12},{13,14},{2,1},{4,3},{6,5},{... | collective-permute-start | bytes 1179656 | tf_op jit(solution)/shard_map/ppermute | solution.py:570
